TPU v7x, 128 devices: a whole 4x4x4 slice. The times are simulated.
128 devices in a mesh: req: 4 (over z), tile: 8 (over y, core), span: 4 (over x).
Axes of the slice: x: 4, y: 4, z: 4, core: 2. Of those that a mesh axis runs over, the one named last changes fastest.
Arguments:
- latents: bfloat16 [32, 64, 128, 512], P(('req', 'span'), 'tile'), may hold values from -12 to 12
- frame_counts: int32 [4], replicated, may hold values from 1 to 16, 32 in all
- norm_gain: float32 [512], replicated, may hold values from 0.1 to 1.9
- norm_shift: float32 [512], replicated, may hold values from -3 to 3
- conv_weight: bfloat16 [3, 3, 3, 512, 512], replicated, may hold values from -0.0546875 to 0.0546875
- conv_bias: float32 [512], replicated, may hold values from -2 to 2
Outputs:
- decoded: bfloat16 [32, 64, 128, 512], P(('req', 'span'), 'tile')
Inputs may be any that keep to these rules, and one draw needn't show every extreme that they name: `frame_counts`: the 4 counts sum to 32, and the largest is exactly 16.
All inputs are finite; a program needn't handle non-finite values.
Results may differ from a plain program's by a relative error of at most 0.0031.
Values may be sent and summed in bfloat16 or wider, within the bound.
No kernel may reach another device: no remote copies, remote signals or barrier semaphores. Data moves between devices by JAX's collectives and lax.ppermute only.
A program may use at most 192 MiB of HBM per device.

v0:
```python
import jax
import jax.numpy as jnp
from jax import lax
from jax.sharding import PartitionSpec as P

GROUPS = 32


EPSILON = 1e-06


def extended_2(array, sides, width):
    for axis, dim in sides:
        count, length = (lax.axis_size(axis), array.shape[dim])
        up = [(i, (i + 1) % count) for i in range(count - 1)]
        down = [(j, i) for i, j in up]
        last = lax.slice_in_dim(array, length - width, length, axis=dim)
        leading = lax.slice_in_dim(array, 0, width, axis=dim)
        before = lax.ppermute(last, axis, up)
        after = lax.ppermute(leading, axis, down)
        array = jnp.concatenate([before, array, after], axis=dim)
    return array


def shifted(array, axis, by):
    count = lax.axis_size(axis)
    pairs = [(i, i + by) for i in range(count) if 0 <= i + by < count]
    return lax.ppermute(array, axis, pairs)


def membership(positions, request_start, request_end):
    return (positions[:, None] >= request_start[None, :]) & (
        positions[:, None] < request_end[None, :]
    )


def normalize(
    source, positions, request_start, request_end, group_mean, group_scale, norm_gain, norm_shift
):
    inside = membership(positions, request_start, request_end).astype(jnp.float32)
    per_group = source.shape[-1] // group_mean.shape[1]
    frame_mean = jnp.repeat(
        jnp.dot(inside, group_mean, precision=lax.Precision.HIGHEST), per_group, axis=1
    )
    frame_scale = jnp.repeat(
        jnp.dot(inside, group_scale, precision=lax.Precision.HIGHEST), per_group, axis=1
    )
    centred = (source.astype(jnp.float32) - frame_mean[:, None, None, :]) * frame_scale[
        :, None, None, :
    ]
    return jax.nn.silu(centred * norm_gain + norm_shift).astype(jnp.bfloat16)


def finish_stats(local_sums, local_squares, cell_count):
    total_sums, total_squares = lax.psum((local_sums, local_squares), ("req", "tile", "span"))
    group_mean = total_sums / cell_count
    group_scale = lax.rsqrt(total_squares / cell_count - group_mean * group_mean + EPSILON)
    return (group_mean, group_scale)


def extend_rows(source):
    haloed = extended_2(source, (("tile", 1),), 1)
    tile_place = lax.axis_index("tile")
    upper_rim = jnp.where(tile_place == 0, haloed[:, 1:2], haloed[:, 0:1])
    bottom = jnp.where(tile_place == lax.axis_size("tile") - 1, haloed[:, -2:-1], haloed[:, -1:])
    return jnp.concatenate([upper_rim, haloed[:, 1:-1], bottom], axis=1)


def extend_frames(source):
    earlier = shifted(source, ("req", "span"), 1)
    return jnp.concatenate([earlier, source], axis=0)


def extend(source):
    grown = extend_rows(extend_frames(source))
    return grown


def convolve(padded, tap_index, conv_weight, frame_count, row_count, col_count, channels):
    accumulated = jnp.zeros((frame_count * row_count * col_count, channels), jnp.float32)
    for time_tap in range(3):
        chosen = jnp.take(padded, tap_index[time_tap], axis=0)
        for row_tap in range(3):
            stacked = jnp.concatenate(
                [
                    chosen[:, row_tap : row_tap + row_count, col_tap : col_tap + col_count]
                    for col_tap in range(3)
                ],
                axis=-1,
            )
            kernel = conv_weight[time_tap, row_tap].reshape(3 * channels, channels)
            accumulated = accumulated + jnp.dot(
                stacked.reshape(frame_count * row_count * col_count, 3 * channels),
                kernel,
                preferred_element_type=jnp.float32,
            )
    return accumulated.reshape(frame_count, row_count, col_count, channels)


def shards(latents, frame_counts, norm_gain, norm_shift, conv_weight, conv_bias):
    frame_count, row_count, col_count, channels = latents.shape
    per_group = channels // GROUPS
    request_end = jnp.cumsum(frame_counts)
    request_start = request_end - frame_counts
    first_frame = lax.axis_index(("req", "span")) * frame_count
    positions = first_frame + jnp.arange(frame_count, dtype=jnp.int32)
    inside = membership(positions, request_start, request_end)
    values = latents.astype(jnp.float32)
    group_sums = jnp.sum(values, axis=(1, 2)).reshape(frame_count, GROUPS, per_group).sum(-1)
    group_squares = (
        jnp.sum(values * values, axis=(1, 2)).reshape(frame_count, GROUPS, per_group).sum(-1)
    )
    weights_in = inside.astype(jnp.float32)
    local_sums = jnp.dot(weights_in.T, group_sums, precision=lax.Precision.HIGHEST)
    local_squares = jnp.dot(weights_in.T, group_squares, precision=lax.Precision.HIGHEST)
    cell_count = (
        frame_counts * (row_count * lax.axis_size("tile") * col_count * per_group)
    ).astype(jnp.float32)[:, None]
    group_mean, group_scale = finish_stats(local_sums, local_squares, cell_count)
    hidden = normalize(
        latents,
        positions,
        request_start,
        request_end,
        group_mean,
        group_scale,
        norm_gain,
        norm_shift,
    )
    extended = extend(hidden)
    padded = jnp.pad(extended, ((0, 0), (0, 0), (1, 1), (0, 0)), mode="edge")
    frame_start = jnp.sum(jnp.where(inside, request_start[None, :], 0), axis=1)
    tap_index = jnp.stack(
        [
            jnp.maximum(positions - 2 + time_tap, frame_start) - first_frame + 2
            for time_tap in range(3)
        ],
        axis=0,
    )
    conv = convolve(padded, tap_index, conv_weight, frame_count, row_count, col_count, channels)
    return (values + conv + conv_bias).astype(jnp.bfloat16)


def solution(mesh):
    placed = (P(("req", "span"), "tile", None, None), P(), P(), P(), P(), P())
    return jax.shard_map(
        shards,
        mesh=mesh,
        in_specs=placed,
        out_specs=P(("req", "span"), "tile", None, None),
        check_vma=False,
    )
```

profile of v0, /device:TPU:41, one launch (start us, length us, event | category | flops | bytes accessed | tf_op | source)
XLA Modules:
  0.0 287.2 jit_solution(3329410029690608245)
XLA Ops:
  4.6 65.0 %all-reduce = (f32[4,32]{1,0:T(4,128)S(1)}, f32[4,32]{1,0:T(4,128)S(1)}) all-reduce(f32[4,32]{1,0:T(4,128)S(1)} %fusion.40, f32[4,32]{1,0:T(4,128)S(1)} %fusion.39), channel_id=1, replica_groups=mesh['req'=4,'tile'=8,'span'=4] {'req','tile','span'}, use_global_device_ids=true, to_apply=%region_6.7 | all-reduce | flops 256 | bytes 2048 | tf_op jit(solution)/shard_map/psum | solution.py:55
  70.3 3.0 %fusion.24 = bf16[2,8,128,512]{3,2,1,0:T(8,128)(2,1)S(1)} fusion(bf16[2,8,128,512]{3,2,1,0:T(8,128)(2,1)} %param.8, f32[512]{0:T(512)} %param.11, f32[512]{0:T(512)} %param.10, f32[2,512]{1,0:T(2,128)S(1)} %mul.42, f32[2,512]{1,0:T(2,128)S(1)} %sub.34), kind=kLoop, calls=%fused_computation.42 | loop fusion | flops 10485760 | bytes 4206592 | tf_op jit(solution)/shard_map/convert_element_type | solution.py:51
  75.3 48.6 %collective-permute-done = bf16[2,8,128,512]{3,2,1,0:T(8,128)(2,1)} collective-permute-done((bf16[2,8,128,512]{3,2,1,0:T(8,128)(2,1)S(1)}, bf16[2,8,128,512]{3,2,1,0:T(8,128)(2,1)}, u32[]{:S(2)}, u32[]{:S(2)}) %collective-permute-start) | collective-permute-done | bytes 2097184 | tf_op jit(solution)/shard_map/ppermute | solution.py:28
  124.9 4.4 %collective-permute-start.1 = (bf16[4,1,128,512]{3,2,1,0:T(8,128)(2,1)S(1)}, bf16[4,1,128,512]{3,2,1,0:T(8,128)(2,1)S(1)}, u32[]{:S(2)}, u32[]{:S(2)}) collective-permute-start(bf16[4,1,128,512]{3,2,1,0:T(8,128)(2,1)S(1)} %pad_maximum_fusion.9), channel_id=1, source_target_pairs={{0,4},{4,8},{8,12},{12,16},{16,20},{20,24},{24,28},{1,5},{5,9},{9,... | collective-permute-start | bytes 1572872 | tf_op jit(solution)/shard_map/ppermute | solution.py:19
  129.4 6.0 %collective-permute-done.1 = bf16[4,1,128,512]{3,2,1,0:T(8,128)(2,1)S(1)} collective-permute-done((bf16[4,1,128,512]{3,2,1,0:T(8,128)(2,1)S(1)}, bf16[4,1,128,512]{3,2,1,0:T(8,128)(2,1)S(1)}, u32[]{:S(2)}, u32[]{:S(2)}) %collective-permute-start.1) | collective-permute-done | bytes 524320 | tf_op jit(solution)/shard_map/ppermute | solution.py:19
  136.5 3.6 %collective-permute-start.2 = (bf16[4,1,128,512]{3,2,1,0:T(8,128)(2,1)S(1)}, bf16[4,1,128,512]{3,2,1,0:T(8,128)(2,1)S(1)}, u32[]{:S(2)}, u32[]{:S(2)}) collective-permute-start(bf16[4,1,128,512]{3,2,1,0:T(8,128)(2,1)S(1)} %get-tuple-element.19), channel_id=1, source_target_pairs={{4,0},{8,4},{12,8},{16,12},{20,16},{24,20},{28,24},{5,1},{9,5},{13... | collective-permute-start | bytes 1572872 | tf_op jit(solution)/shard_map/ppermute | solution.py:20
  140.1 9.6 %fusion.35 = (bf16[1,1,3,512,512]{4,3,2,1,0:T(8,128)(2,1)}, bf16[1,1,3,512,512]{4,3,2,1,0:T(8,128)(2,1)}, bf16[1,1,3,512,512]{4,3,2,1,0:T(8,128)(2,1)}, bf16[1,1...) fusion(bf16[3,3,3,512,512]{4,3,2,1,0:T(8,128)(2,1)} %param.12), kind=kLoop, calls=%fused_computation.77 | loop fusion | bytes 28311552 | tf_op jit(solution)/shard_map/slice | solution.py:91
  149.8 9.9 %fusion.11 = bf16[4,10,130,512]{3,2,1,0:T(8,128)(2,1)} fusion(bf16[4,1,128,512]{3,2,1,0:T(8,128)(2,1)S(1)} %broadcast_select_fusion.3, bf16[4,1,128,512]{3,2,1,0:T(8,128)(2,1)S(1)} %get-tuple-element.18, bf16[2,8,128,512]{3,2,1,0:T(8,128)(2,1)S(1)} %fusion.24, bf16[2,8,128,512]{3,2,1,0:T(8,128)(2,1)} %collective-permute-done), kind=kLoop, calls=%fused_computation.29 | loop fusion | flops 90521600 | bytes 10567680 | tf_op jit(solution)/shard_map/jit(_pad)/concatenate | solution.py:131
  159.7 3.3 %gather_fusion.2 = bf16[2,10,130,512]{3,2,1,0:T(8,128)(2,1)S(1)} fusion(bf16[4,10,130,512]{3,2,1,0:T(8,128)(2,1)} %fusion.11, s32[1024]{0:T(1024)S(1)} %pad_clamp_fusion), kind=kCustom, calls=%fused_computation.2.clone | custom fusion | bytes 5324808 | tf_op jit(solution)/shard_map/jit(_take)/gather | solution.py:82
  163.0 4.9 %gather_fusion.1 = bf16[2,10,130,512]{3,2,1,0:T(8,128)(2,1)} fusion(bf16[4,10,130,512]{3,2,1,0:T(8,128)(2,1)} %fusion.11, s32[1024]{0:T(1024)S(1)} %pad_clamp_fusion.1), kind=kCustom, calls=%fused_computation.1.clone | custom fusion | bytes 5324808 | tf_op jit(solution)/shard_map/jit(_take)/gather | solution.py:82
  168.0 4.9 %gather_fusion = bf16[2,10,130,512]{3,2,1,0:T(8,128)(2,1)} fusion(bf16[4,10,130,512]{3,2,1,0:T(8,128)(2,1)} %fusion.11, s32[1024]{0:T(1024)S(1)} %pad_clamp_fusion.2), kind=kCustom, calls=%fused_computation.clone | custom fusion | bytes 5324808 | tf_op jit(solution)/shard_map/jit(_take)/gather | solution.py:82
  172.8 2.3 broadcast_select_fusion
  175.2 8.0 %fusion.36 = (bf16[2,8,128,512]{3,2,1,0:T(8,128)(2,1)}, bf16[2,8,128,512]{3,2,1,0:T(8,128)(2,1)}, bf16[2,8,128,512]{3,2,1,0:T(8,128)(2,1)}, bf16[2,8,128,512]{3,...) fusion(bf16[2,10,130,512]{3,2,1,0:T(8,128)(2,1)S(1)} %get-tuple, ...), kind=kLoop, calls=%fused_computation.78 | loop fusion | bytes 37748736 | tf_op jit(solution)/shard_map/slice | solution.py:86
  183.5 6.8 %fusion.37 = (bf16[2,8,128,512]{3,2,1,0:T(8,128)(2,1)S(1)}, bf16[2,8,128,512]{3,2,1,0:T(8,128)(2,1)}, bf16[2,8,128,512]{3,2,1,0:T(8,128)(2,1)}, bf16[2,8,128,512...) fusion(bf16[2,10,130,512]{3,2,1,0:T(8,128)(2,1)S(1)} %broadcast, ...), kind=kLoop, calls=%fused_computation.79 | loop fusion | bytes 37748736 | tf_op jit(solution)/shard_map/slice | solution.py:86
  190.3 7.1 %fusion.38 = (bf16[2,8,128,512]{3,2,1,0:T(8,128)(2,1)}, bf16[2,8,128,512]{3,2,1,0:T(8,128)(2,1)}, bf16[2,8,128,512]{3,2,1,0:T(8,128)(2,1)}, bf16[2,8,128,512]{3,...) fusion(bf16[2,10,130,512]{3,2,1,0:T(8,128)(2,1)S(1)} %get-tuple, ...), kind=kLoop, calls=%fused_computation.80 | loop fusion | bytes 37748736 | tf_op jit(solution)/shard_map/slice | solution.py:86
  197.4 3.7 %pad_maximum_fusion.7 = bf16[2,8,128,1536]{3,2,1,0:T(8,128)(2,1)S(1)} fusion(bf16[2,8,128,512]{3,2,1,0:T(8,128)(2,1)} %get-tuple-element.32, bf16[2,8,128,512]{3,2,1,0:T(8,128)(2,1)} %get-tuple-element.33, bf16[2,8,128,512]{3,2,1,0:T(8,128)(2,1)} %get-tuple-element.34), kind=kLoop, calls=%fused_computation.24 | loop fusion | flops 18874368 | bytes 12582912 | tf_op jit(solution)/shard_map/concatenate | solution.py:84
  201.1 4.9 %fusion.48 = f32[2048,512]{1,0:T(8,128)} fusion(bf16[2048,1536]{1,0:T(8,128)(2,1)S(1)} %bitcast.49, bf16[1536,512]{1,0:T(8,128)(2,1)S(1)} %bitcast.64), kind=kOutput, calls=%fused_computation.90 | convolution fusion | flops 3221225472 | bytes 12058624 | tf_op jit(solution)/shard_map/dot_general | solution.py:92
  206.0 4.4 %pad_maximum_fusion.6 = bf16[2,8,128,1536]{3,2,1,0:T(8,128)(2,1)S(1)} fusion(bf16[2,8,128,512]{3,2,1,0:T(8,128)(2,1)S(1)} %copy-done.17, bf16[2,8,128,512]{3,2,1,0:T(8,128)(2,1)S(1)} %copy-done.18, bf16[2,8,128,512]{3,2,1,0:T(8,128)(2,1)S(1)} %copy-done.19), kind=kLoop, calls=%fused_computation.23 | loop fusion | flops 18874368 | bytes 12582912 | tf_op jit(solution)/shard_map/concatenate | solution.py:84
  210.5 4.9 %fusion.47 = f32[2048,512]{1,0:T(8,128)} fusion(bf16[2048,1536]{1,0:T(8,128)(2,1)S(1)} %bitcast.50, bf16[1536,512]{1,0:T(8,128)(2,1)S(1)} %bitcast.63), kind=kOutput, calls=%fused_computation.89 | convolution fusion | flops 3221225472 | bytes 12058624 | tf_op jit(solution)/shard_map/dot_general | solution.py:92
  216.8 4.9 %fusion.41 = f32[2048,512]{1,0:T(8,128)} fusion(bf16[2048,1536]{1,0:T(8,128)(2,1)S(1)} %bitcast.56, bf16[1536,512]{1,0:T(8,128)(2,1)S(1)} %bitcast.62), kind=kOutput, calls=%fused_computation.83 | convolution fusion | flops 3221225472 | bytes 12058624 | tf_op jit(solution)/shard_map/dot_general | solution.py:92
  221.7 4.9 %fusion.42 = f32[2048,512]{1,0:T(8,128)} fusion(bf16[2048,1536]{1,0:T(8,128)(2,1)S(1)} %bitcast.55, bf16[1536,512]{1,0:T(8,128)(2,1)S(1)} %bitcast.61), kind=kOutput, calls=%fused_computation.84 | convolution fusion | flops 3221225472 | bytes 12058624 | tf_op jit(solution)/shard_map/dot_general | solution.py:92
  226.6 4.2 %pad_maximum_fusion.2 = bf16[2,8,128,1536]{3,2,1,0:T(8,128)(2,1)S(1)} fusion(bf16[2,8,128,512]{3,2,1,0:T(8,128)(2,1)S(1)} %copy-done.14, bf16[2,8,128,512]{3,2,1,0:T(8,128)(2,1)S(1)} %copy-done.15, bf16[2,8,128,512]{3,2,1,0:T(8,128)(2,1)S(1)} %copy-done.16), kind=kLoop, calls=%fused_computation.19 | loop fusion | flops 18874368 | bytes 12582912 | tf_op jit(solution)/shard_map/concatenate | solution.py:84
  230.9 4.9 %fusion.43 = f32[2048,512]{1,0:T(8,128)} fusion(bf16[2048,1536]{1,0:T(8,128)(2,1)S(1)} %bitcast.51, bf16[1536,512]{1,0:T(8,128)(2,1)S(1)} %bitcast.60), kind=kOutput, calls=%fused_computation.85 | convolution fusion | flops 3221225472 | bytes 12058624 | tf_op jit(solution)/shard_map/dot_general | solution.py:92
  235.8 4.2 %pad_maximum_fusion.3 = bf16[2,8,128,1536]{3,2,1,0:T(8,128)(2,1)S(1)} fusion(bf16[2,8,128,512]{3,2,1,0:T(8,128)(2,1)S(1)} %copy-done.12, bf16[2,8,128,512]{3,2,1,0:T(8,128)(2,1)S(1)} %copy-done.13, bf16[2,8,128,512]{3,2,1,0:T(8,128)(2,1)S(1)} %copy-done.11), kind=kLoop, calls=%fused_computation.20 | loop fusion | flops 18874368 | bytes 12582912 | tf_op jit(solution)/shard_map/concatenate | solution.py:84
  240.1 4.9 %fusion.44 = f32[2048,512]{1,0:T(8,128)} fusion(bf16[2048,1536]{1,0:T(8,128)(2,1)S(1)} %bitcast.52, bf16[1536,512]{1,0:T(8,128)(2,1)S(1)} %bitcast.59), kind=kOutput, calls=%fused_computation.86 | convolution fusion | flops 3221225472 | bytes 12058624 | tf_op jit(solution)/shard_map/dot_general | solution.py:92
  245.1 4.2 %pad_maximum_fusion.5 = bf16[2,8,128,1536]{3,2,1,0:T(8,128)(2,1)S(1)} fusion(bf16[2,8,128,512]{3,2,1,0:T(8,128)(2,1)S(1)} %copy-done.8, bf16[2,8,128,512]{3,2,1,0:T(8,128)(2,1)S(1)} %copy-done.9, bf16[2,8,128,512]{3,2,1,0:T(8,128)(2,1)S(1)} %copy-done.10), kind=kLoop, calls=%fused_computation.22 | loop fusion | flops 18874368 | bytes 12582912 | tf_op jit(solution)/shard_map/concatenate | solution.py:84
  249.3 4.9 %fusion.46 = f32[2048,512]{1,0:T(8,128)} fusion(bf16[2048,1536]{1,0:T(8,128)(2,1)S(1)} %bitcast.53, bf16[1536,512]{1,0:T(8,128)(2,1)S(1)} %bitcast.58), kind=kOutput, calls=%fused_computation.88 | convolution fusion | flops 3221225472 | bytes 12058624 | tf_op jit(solution)/shard_map/dot_general | solution.py:92
  254.3 4.5 %pad_maximum_fusion.4 = bf16[2,8,128,1536]{3,2,1,0:T(8,128)(2,1)S(1)} fusion(bf16[2,8,128,512]{3,2,1,0:T(8,128)(2,1)S(1)} %get-tuple-element.51, bf16[2,8,128,512]{3,2,1,0:T(8,128)(2,1)S(1)} %copy-done.6, bf16[2,8,128,512]{3,2,1,0:T(8,128)(2,1)S(1)} %copy-done.7), kind=kLoop, calls=%fused_computation.21 | loop fusion | flops 18874368 | bytes 12582912 | tf_op jit(solution)/shard_map/concatenate | solution.py:84
  258.8 5.0 %fusion.45 = f32[2048,512]{1,0:T(8,128)} fusion(bf16[2048,1536]{1,0:T(8,128)(2,1)S(1)} %bitcast.54, bf16[1536,512]{1,0:T(8,128)(2,1)S(1)} %bitcast.57), kind=kOutput, calls=%fused_computation.87 | convolution fusion | flops 3221225472 | bytes 12058624 | tf_op jit(solution)/shard_map/dot_general | solution.py:92
  263.8 4.2 %pad_maximum_fusion.8 = bf16[2,8,128,1536]{3,2,1,0:T(8,128)(2,1)S(1)} fusion(bf16[2,8,128,512]{3,2,1,0:T(8,128)(2,1)S(1)} %copy-done.4, bf16[2,8,128,512]{3,2,1,0:T(8,128)(2,1)S(1)} %copy-done.5, bf16[2,8,128,512]{3,2,1,0:T(8,128)(2,1)S(1)} %copy-done.3), kind=kLoop, calls=%fused_computation.25 | loop fusion | flops 18874368 | bytes 12582912 | tf_op jit(solution)/shard_map/concatenate | solution.py:84
  268.0 14.8 %add_add_fusion = f32[2048,512]{1,0:T(8,128)} fusion(f32[2048,512]{1,0:T(8,128)} %fusion.48, f32[2048,512]{1,0:T(8,128)} %fusion.47, f32[2048,512]{1,0:T(8,128)} %fusion.46, f32[2048,512]{1,0:T(8,128)} %fusion.45, f32[2048,512]{1,0:T(8,128)} %fusion.44, f32[2048,512]{1,0:T(8,128)} %fusion.43, f32[2048,512]{1,0:T(8,128)} %fusion.41, ...), kind=kOutput, calls=%fused_computation.46 | convolution fusion | flops 3229614080 | bytes 45613056 | tf_op jit(solution)/shard_map/dot_general | solution.py:92
  282.8 4.4 %fusion.27 = bf16[2,8,128,512]{3,2,1,0:T(8,128)(2,1)} fusion(f32[2,8,128,512]{3,2,1,0:T(8,128)} %bitcast.47, bf16[2,8,128,512]{3,2,1,0:T(8,128)(2,1)S(1)} %copy-done, f32[512]{0:T(512)S(1)} %copy-done.28), kind=kLoop, calls=%fused_computation.45 | loop fusion | flops 4194304 | bytes 8390656 | tf_op jit(solution)/shard_map/convert_element_type | solution.py:141
  (86 shorter events, 11.2 us)
Async XLA Ops:
  73.4 50.6 %collective-permute-start = (bf16[2,8,128,512]{3,2,1,0:T(8,128)(2,1)S(1)}, bf16[2,8,128,512]{3,2,1,0:T(8,128)(2,1)}, u32[]{:S(2)}, u32[]{:S(2)}) collective-permute-start(bf16[2,8,128,512]{3,2,1,0:T(8,128)(2,1)S(1)} %fusion.24), channel_id=1, source_target_pairs={{0,1},{1,2},{2,3},{3,32},{32,33},{33,34},{34,35},{35,64},{64,65},{... | collective-permute-start | bytes 6291464 | tf_op jit(solution)/shard_map/ppermute | solution.py:28
  124.9 10.5 %collective-permute-start.1 = (bf16[4,1,128,512]{3,2,1,0:T(8,128)(2,1)S(1)}, bf16[4,1,128,512]{3,2,1,0:T(8,128)(2,1)S(1)}, u32[]{:S(2)}, u32[]{:S(2)}) collective-permute-start(bf16[4,1,128,512]{3,2,1,0:T(8,128)(2,1)S(1)} %pad_maximum_fusion.9), channel_id=1, source_target_pairs={{0,4},{4,8},{8,12},{12,16},{16,20},{20,24},{24,28},{1,5},{5,9},{9,... | collective-permute-start | bytes 1572872 | tf_op jit(solution)/shard_map/ppermute | solution.py:19
  136.5 13.2 %collective-permute-start.2 = (bf16[4,1,128,512]{3,2,1,0:T(8,128)(2,1)S(1)}, bf16[4,1,128,512]{3,2,1,0:T(8,128)(2,1)S(1)}, u32[]{:S(2)}, u32[]{:S(2)}) collective-permute-start(bf16[4,1,128,512]{3,2,1,0:T(8,128)(2,1)S(1)} %get-tuple-element.19), channel_id=1, source_target_pairs={{4,0},{8,4},{12,8},{16,12},{20,16},{24,20},{28,24},{5,1},{9,5},{13... | collective-permute-start | bytes 1572872 | tf_op jit(solution)/shard_map/ppermute | solution.py:20
  175.2 8.0 %copy-start.1 = (bf16[2,10,130,512]{3,2,1,0:T(8,128)(2,1)S(1)}, bf16[2,10,130,512]{3,2,1,0:T(8,128)(2,1)}, u32[]{:S(2)}) copy-start(bf16[2,10,130,512]{3,2,1,0:T(8,128)(2,1)} %gather_fusion) | copy-start | bytes 7987204
  197.4 3.7 %copy-start.27 = (bf16[1,1,3,512,512]{4,3,2,1,0:T(8,128)(2,1)S(1)}, bf16[1,1,3,512,512]{4,3,2,1,0:T(8,128)(2,1)}, u32[]{:S(2)}) copy-start(bf16[1,1,3,512,512]{4,3,2,1,0:T(8,128)(2,1)} %get-tuple-element.28) | copy-start | bytes 4718596
  201.1 4.9 %copy-start.17 = (bf16[2,8,128,512]{3,2,1,0:T(8,128)(2,1)S(1)}, bf16[2,8,128,512]{3,2,1,0:T(8,128)(2,1)}, u32[]{:S(2)}) copy-start(bf16[2,8,128,512]{3,2,1,0:T(8,128)(2,1)} %get-tuple-element.35) | copy-start | bytes 6291460
  201.1 4.9 %copy-start.18 = (bf16[2,8,128,512]{3,2,1,0:T(8,128)(2,1)S(1)}, bf16[2,8,128,512]{3,2,1,0:T(8,128)(2,1)}, u32[]{:S(2)}) copy-start(bf16[2,8,128,512]{3,2,1,0:T(8,128)(2,1)} %get-tuple-element.36) | copy-start | bytes 6291460
  201.1 4.9 %copy-start.19 = (bf16[2,8,128,512]{3,2,1,0:T(8,128)(2,1)S(1)}, bf16[2,8,128,512]{3,2,1,0:T(8,128)(2,1)}, u32[]{:S(2)}) copy-start(bf16[2,8,128,512]{3,2,1,0:T(8,128)(2,1)} %get-tuple-element.37) | copy-start | bytes 6291460
  206.0 4.5 %copy-start.26 = (bf16[1,1,3,512,512]{4,3,2,1,0:T(8,128)(2,1)S(1)}, bf16[1,1,3,512,512]{4,3,2,1,0:T(8,128)(2,1)}, u32[]{:S(2)}) copy-start(bf16[1,1,3,512,512]{4,3,2,1,0:T(8,128)(2,1)} %get-tuple-element.21) | copy-start | bytes 4718596
  210.5 4.9 %copy-start.2 = (bf16[2,8,128,512]{3,2,1,0:T(8,128)(2,1)S(1)}, bf16[2,8,128,512]{3,2,1,0:T(8,128)(2,1)}, u32[]{:S(2)}) copy-start(bf16[2,8,128,512]{3,2,1,0:T(8,128)(2,1)} %get-tuple-element.46) | copy-start | bytes 6291460
  215.4 1.4 copy-start.25
  216.8 4.9 %copy-start.24 = (bf16[1,1,3,512,512]{4,3,2,1,0:T(8,128)(2,1)S(1)}, bf16[1,1,3,512,512]{4,3,2,1,0:T(8,128)(2,1)}, u32[]{:S(2)}) copy-start(bf16[1,1,3,512,512]{4,3,2,1,0:T(8,128)(2,1)} %get-tuple-element.26) | copy-start | bytes 4718596
  221.7 4.9 %copy-start.14 = (bf16[2,8,128,512]{3,2,1,0:T(8,128)(2,1)S(1)}, bf16[2,8,128,512]{3,2,1,0:T(8,128)(2,1)}, u32[]{:S(2)}) copy-start(bf16[2,8,128,512]{3,2,1,0:T(8,128)(2,1)} %get-tuple-element.39) | copy-start | bytes 6291460
  221.7 4.9 %copy-start.15 = (bf16[2,8,128,512]{3,2,1,0:T(8,128)(2,1)S(1)}, bf16[2,8,128,512]{3,2,1,0:T(8,128)(2,1)}, u32[]{:S(2)}) copy-start(bf16[2,8,128,512]{3,2,1,0:T(8,128)(2,1)} %get-tuple-element.40) | copy-start | bytes 6291460
  221.7 4.9 %copy-start.16 = (bf16[2,8,128,512]{3,2,1,0:T(8,128)(2,1)S(1)}, bf16[2,8,128,512]{3,2,1,0:T(8,128)(2,1)}, u32[]{:S(2)}) copy-start(bf16[2,8,128,512]{3,2,1,0:T(8,128)(2,1)} %get-tuple-element.41) | copy-start | bytes 6291460
  226.6 4.2 %copy-start.23 = (bf16[1,1,3,512,512]{4,3,2,1,0:T(8,128)(2,1)S(1)}, bf16[1,1,3,512,512]{4,3,2,1,0:T(8,128)(2,1)}, u32[]{:S(2)}) copy-start(bf16[1,1,3,512,512]{4,3,2,1,0:T(8,128)(2,1)} %get-tuple-element.25) | copy-start | bytes 4718596
  230.9 4.9 %copy-start.11 = (bf16[2,8,128,512]{3,2,1,0:T(8,128)(2,1)S(1)}, bf16[2,8,128,512]{3,2,1,0:T(8,128)(2,1)}, u32[]{:S(2)}) copy-start(bf16[2,8,128,512]{3,2,1,0:T(8,128)(2,1)} %get-tuple-element.47) | copy-start | bytes 6291460
  230.9 4.9 %copy-start.12 = (bf16[2,8,128,512]{3,2,1,0:T(8,128)(2,1)S(1)}, bf16[2,8,128,512]{3,2,1,0:T(8,128)(2,1)}, u32[]{:S(2)}) copy-start(bf16[2,8,128,512]{3,2,1,0:T(8,128)(2,1)} %get-tuple-element.54) | copy-start | bytes 6291460
  230.9 4.9 %copy-start.13 = (bf16[2,8,128,512]{3,2,1,0:T(8,128)(2,1)S(1)}, bf16[2,8,128,512]{3,2,1,0:T(8,128)(2,1)}, u32[]{:S(2)}) copy-start(bf16[2,8,128,512]{3,2,1,0:T(8,128)(2,1)} %get-tuple-element.55) | copy-start | bytes 6291460
  235.8 4.2 %copy-start.22 = (bf16[1,1,3,512,512]{4,3,2,1,0:T(8,128)(2,1)S(1)}, bf16[1,1,3,512,512]{4,3,2,1,0:T(8,128)(2,1)}, u32[]{:S(2)}) copy-start(bf16[1,1,3,512,512]{4,3,2,1,0:T(8,128)(2,1)} %get-tuple-element.24) | copy-start | bytes 4718596
  240.1 5.0 %copy-start.8 = (bf16[2,8,128,512]{3,2,1,0:T(8,128)(2,1)S(1)}, bf16[2,8,128,512]{3,2,1,0:T(8,128)(2,1)}, u32[]{:S(2)}) copy-start(bf16[2,8,128,512]{3,2,1,0:T(8,128)(2,1)} %get-tuple-element.48) | copy-start | bytes 6291460
  240.1 5.0 %copy-start.9 = (bf16[2,8,128,512]{3,2,1,0:T(8,128)(2,1)S(1)}, bf16[2,8,128,512]{3,2,1,0:T(8,128)(2,1)}, u32[]{:S(2)}) copy-start(bf16[2,8,128,512]{3,2,1,0:T(8,128)(2,1)} %get-tuple-element.49) | copy-start | bytes 6291460
  240.1 5.0 %copy-start.10 = (bf16[2,8,128,512]{3,2,1,0:T(8,128)(2,1)S(1)}, bf16[2,8,128,512]{3,2,1,0:T(8,128)(2,1)}, u32[]{:S(2)}) copy-start(bf16[2,8,128,512]{3,2,1,0:T(8,128)(2,1)} %get-tuple-element.50) | copy-start | bytes 6291460
  245.1 4.2 %copy-start.21 = (bf16[1,1,3,512,512]{4,3,2,1,0:T(8,128)(2,1)S(1)}, bf16[1,1,3,512,512]{4,3,2,1,0:T(8,128)(2,1)}, u32[]{:S(2)}) copy-start(bf16[1,1,3,512,512]{4,3,2,1,0:T(8,128)(2,1)} %get-tuple-element.22) | copy-start | bytes 4718596
  249.3 5.0 %copy-start.6 = (bf16[2,8,128,512]{3,2,1,0:T(8,128)(2,1)S(1)}, bf16[2,8,128,512]{3,2,1,0:T(8,128)(2,1)}, u32[]{:S(2)}) copy-start(bf16[2,8,128,512]{3,2,1,0:T(8,128)(2,1)} %get-tuple-element.52) | copy-start | bytes 6291460
  249.3 4.9 %copy-start.7 = (bf16[2,8,128,512]{3,2,1,0:T(8,128)(2,1)S(1)}, bf16[2,8,128,512]{3,2,1,0:T(8,128)(2,1)}, u32[]{:S(2)}) copy-start(bf16[2,8,128,512]{3,2,1,0:T(8,128)(2,1)} %get-tuple-element.53) | copy-start | bytes 6291460
  254.3 4.5 %copy-start.20 = (bf16[1,1,3,512,512]{4,3,2,1,0:T(8,128)(2,1)S(1)}, bf16[1,1,3,512,512]{4,3,2,1,0:T(8,128)(2,1)}, u32[]{:S(2)}) copy-start(bf16[1,1,3,512,512]{4,3,2,1,0:T(8,128)(2,1)} %get-tuple-element.23) | copy-start | bytes 4718596
  258.8 5.0 %copy-start.3 = (bf16[2,8,128,512]{3,2,1,0:T(8,128)(2,1)S(1)}, bf16[2,8,128,512]{3,2,1,0:T(8,128)(2,1)}, u32[]{:S(2)}) copy-start(bf16[2,8,128,512]{3,2,1,0:T(8,128)(2,1)} %get-tuple-element.29) | copy-start | bytes 6291460
  258.8 5.0 %copy-start.4 = (bf16[2,8,128,512]{3,2,1,0:T(8,128)(2,1)S(1)}, bf16[2,8,128,512]{3,2,1,0:T(8,128)(2,1)}, u32[]{:S(2)}) copy-start(bf16[2,8,128,512]{3,2,1,0:T(8,128)(2,1)} %get-tuple-element.30) | copy-start | bytes 6291460
  258.8 5.0 %copy-start.5 = (bf16[2,8,128,512]{3,2,1,0:T(8,128)(2,1)S(1)}, bf16[2,8,128,512]{3,2,1,0:T(8,128)(2,1)}, u32[]{:S(2)}) copy-start(bf16[2,8,128,512]{3,2,1,0:T(8,128)(2,1)} %get-tuple-element.31) | copy-start | bytes 6291460
  268.0 14.8 %copy-start = (bf16[2,8,128,512]{3,2,1,0:T(8,128)(2,1)S(1)}, bf16[2,8,128,512]{3,2,1,0:T(8,128)(2,1)}, u32[]{:S(2)}) copy-start(bf16[2,8,128,512]{3,2,1,0:T(8,128)(2,1)} %param.8) | copy-start | bytes 6291460
  268.0 14.8 %copy-start.28 = (f32[512]{0:T(512)S(1)}, f32[512]{0:T(512)}, u32[]{:S(2)}) copy-start(f32[512]{0:T(512)} %param.13) | copy-start | bytes 6148
where the time goes:
time: 288 us; the launch traced here: 287 us
  blocking collectives  65 us (23%)
  other arithmetic  56.8 us (20%)
  matrix products  54.9 us (19%)
  waiting for transfers between devices  54.7 us (19%)
  local copies, waits for them, and re-layouts  45.4 us (16%)
  starting transfers between devices  10 us (3%)
    psum x1, blocking collectives, finish_stats(): lax.psum((local_sums, local_squares), ('req', 'tile', 'span'))  65 us
    dot_general x9, matrix products, convolve(): jnp.dot(stacked.reshape(frame_count * row_count * col_count, 3 * channels...  54.1 us
    ppermute x1, waiting for transfers between devices, shifted(): return lax.ppermute(array, axis, pairs)  48.6 us
    concatenate x8, other arithmetic, convolve(): jnp.concatenate([chosen[:, row_tap:row_tap + row_count, col_tap:col_tap +...  30.7 us
    slice x3, local copies, waits for them, and re-layouts, convolve(): chosen[:, row_tap:row_tap + row_count, col_tap:col_tap + col_count]  21.8 us
    gather x3, local copies, waits for them, and re-layouts, convolve(): chosen = jnp.take(padded, tap_index[time_tap], axis=0)  13.1 us
    concatenate x1, other arithmetic, shards(): padded = jnp.pad(extended, ((0, 0), (0, 0), (1, 1), (0, 0)), mode='edge')  9.92 us
    slice x1, local copies, waits for them, and re-layouts, convolve(): kernel = conv_weight[time_tap, row_tap].reshape(3 * channels, channels)  9.58 us
  transfers between devices with their start and end apart: 3, of which 2 were waited for; matrix products, arithmetic and copies ran while one was open for 3% of the time, Pallas kernels for 0%

commit v1 on v0

v1 whole, which is shorter than its diff:
```python
import functools

import jax
import jax.numpy as jnp
from jax import lax
from jax.experimental import pallas as pl
from jax.experimental.pallas import tpu as pltpu
from jax.sharding import PartitionSpec as P

GROUPS = 32
EPSILON = 1e-06
LANES = 128
HIGHEST = lax.Precision.HIGHEST

REQ_OF = 0
SOURCE_0 = 4
SOURCE_1 = 6
IS_TOP = 8
IS_BOTTOM = 9
CORE = 10
COUNTS = 11


def group_matrix(channels, per_group, transpose):
    shape = (LANES, channels) if transpose else (channels, LANES)
    lane = lax.broadcasted_iota(jnp.int32, shape, 0 if transpose else 1)
    channel = lax.broadcasted_iota(jnp.int32, shape, 1 if transpose else 0)
    return (channel // per_group == lane).astype(jnp.float32)


def stats_kernel(per_group, scalars, x_ref, out_ref):
    frame = pl.program_id(0)
    rows, cols, channels = x_ref.shape[1:]

    def one_row(i, carry):
        total, squares = carry
        v = x_ref[0, i].astype(jnp.float32).reshape(cols // 8, 8, channels)
        return total + jnp.sum(v, axis=0), squares + jnp.sum(v * v, axis=0)

    zero = jnp.zeros((8, channels), jnp.float32)
    total, squares = lax.fori_loop(0, rows, one_row, (zero, zero))
    members = group_matrix(channels, per_group, False)
    grouped = [
        jnp.sum(
            lax.dot(part, members, precision=HIGHEST, preferred_element_type=jnp.float32),
            axis=0,
            keepdims=True,
        )
        for part in (total, squares)
    ]
    row = lax.broadcasted_iota(jnp.int32, (8, LANES), 0)
    request = scalars[REQ_OF + 2 + frame]
    mine = jnp.where(row == request, grouped[0], 0.0) + jnp.where(
        row == request + 4, grouped[1], 0.0
    )

    @pl.when(frame == 0)
    def _():
        out_ref[...] = mine

    @pl.when(frame != 0)
    def _():
        out_ref[...] += mine


def local_stats(scalars, latents, per_group):
    frames, rows, cols, channels = latents.shape
    return pl.pallas_call(
        functools.partial(stats_kernel, per_group),
        grid_spec=pltpu.PrefetchScalarGridSpec(
            num_scalar_prefetch=1,
            grid=(frames,),
            in_specs=[pl.BlockSpec((1, rows, cols, channels), lambda f, s: (f, 0, 0, 0))],
            out_specs=pl.BlockSpec((8, LANES), lambda f, s: (0, 0)),
        ),
        out_shape=jax.ShapeDtypeStruct((8, LANES), jnp.float32),
        name="local_stats",
    )(scalars, latents)


def affine_of(scalars, total, gain, shift, cells_per_frame, per_group):
    channels = gain.shape[1]
    row = lax.broadcasted_iota(jnp.int32, (4, LANES), 0)
    frames = jnp.zeros((4, LANES), jnp.float32)
    for r in range(4):
        frames = jnp.where(row == r, scalars[COUNTS + r].astype(jnp.float32), frames)
    cells = frames * float(cells_per_frame)
    mean = total[0:4] / cells
    scale = lax.rsqrt(total[4:8] / cells - mean * mean + EPSILON)
    spread = group_matrix(channels, per_group, True)
    both = lax.dot(
        jnp.concatenate([mean, scale], axis=0),
        spread,
        precision=HIGHEST,
        preferred_element_type=jnp.float32,
    )
    factor = both[4:8] * gain
    return jnp.concatenate([factor, shift - both[0:4] * factor], axis=0)


def normalize_rows(raw, stacked, slot, rows, factor, term):
    cols, channels = raw.shape[2:]
    place = lax.broadcasted_iota(jnp.int32, (cols, channels), 0)
    for i in rows:
        u = raw[slot, i].astype(jnp.float32) * factor + term
        h = u * jnp.tanh(u) + u
        left = jnp.where(place == 0, h, pltpu.roll(h, 1, 0))
        right = jnp.where(place == cols - 1, h, pltpu.roll(h, cols - 1, 0))
        stacked[slot, i, :, 0:channels] = left.astype(jnp.bfloat16)
        stacked[slot, i, :, channels : 2 * channels] = h.astype(jnp.bfloat16)
        stacked[slot, i, :, 2 * channels :] = right.astype(jnp.bfloat16)


def conv_kernel(stage, cells_per_frame, per_group, *refs):
    refs = list(refs)
    take = lambda n: [refs.pop(0) for _ in range(n)]
    (scalars,) = take(1)
    lat, top, bottom = take(3)
    rem, edge, inner = take(3) if stage != "a" else (None, None, None)
    (weight,) = take(1)
    if stage == "a":
        total_ref, gain_ref, shift_ref = take(3)
        affine_out, acc_out = take(2)
    elif stage == "b":
        affine_in, bias_ref, acc_in = take(3)
        acc_out, decoded = take(2)
    else:
        affine_in, bias_ref, acc_in, _ = take(4)
        (decoded,) = take(1)
    raw, stacked, kernels, acc, affine, out_tile, io_sem, w_sem = refs
    rows, cols, channels = lat.shape[1:]
    cells = rows * cols

    if stage == "a":
        sources = [2, 3]
        local_only = True
        second = scalars[SOURCE_1 + 1] - 2
        plan = [(0, 2, 0), (1, 2, 1), (1, 1, second)]
    elif stage == "b":
        sources = [scalars[SOURCE_0 + 1], scalars[SOURCE_1]]
        local_only = False
        plan = [(0, 1, 0), (1, 0, 1)]
    else:
        sources = [scalars[SOURCE_0]]
        local_only = False
        plan = [(0, 0, 0)]

    is_top = scalars[IS_TOP] == 1
    is_bottom = scalars[IS_BOTTOM] == 1
    first_core = scalars[CORE] == 0

    def copy(src, dst, sem):
        return pltpu.make_async_copy(src, dst, sem)

    def pick(cond, yes, no):
        @pl.when(cond)
        def _():
            yes()

        @pl.when(jnp.logical_not(cond))
        def _():
            no()

    def load(slot, frame):
        main, upper, lower = (raw.at[slot, pl.ds(1, rows)], raw.at[slot, 0], raw.at[slot, rows + 1])
        sems = (io_sem.at[slot, 0], io_sem.at[slot, 1], io_sem.at[slot, 2])

        def from_local():
            k = frame - 2
            copy(lat.at[k], main, sems[0]).start()
            pick(
                is_top,
                lambda: copy(lat.at[k, 0], upper, sems[1]).start(),
                lambda: copy(top.at[k], upper, sems[1]).start(),
            )
            pick(
                is_bottom,
                lambda: copy(lat.at[k, rows - 1], lower, sems[2]).start(),
                lambda: copy(bottom.at[k], lower, sems[2]).start(),
            )

        def from_remote():
            copy(rem.at[frame], main, sems[0]).start()
            pick(
                is_top,
                lambda: copy(rem.at[frame, 0], upper, sems[1]).start(),
                lambda: pick(
                    first_core,
                    lambda: copy(edge.at[frame], upper, sems[1]).start(),
                    lambda: copy(inner.at[frame], upper, sems[1]).start(),
                ),
            )
            pick(
                is_bottom,
                lambda: copy(rem.at[frame, rows - 1], lower, sems[2]).start(),
                lambda: pick(
                    first_core,
                    lambda: copy(inner.at[frame], lower, sems[2]).start(),
                    lambda: copy(edge.at[frame], lower, sems[2]).start(),
                ),
            )

        if local_only:
            from_local()
        else:
            pick(frame >= 2, from_local, from_remote)

    def loaded(slot):
        main, upper, lower = (raw.at[slot, pl.ds(1, rows)], raw.at[slot, 0], raw.at[slot, rows + 1])
        copy(lat.at[0], main, io_sem.at[slot, 0]).wait()
        copy(top.at[0], upper, io_sem.at[slot, 1]).wait()
        copy(top.at[0], lower, io_sem.at[slot, 2]).wait()

    load(0, sources[0])
    blocks = []
    for _, a, _ in plan:
        for b in range(3):
            if (a, b) not in blocks:
                blocks.append((a, b))
    copies = []
    for k, (a, b) in enumerate(blocks):
        copies.append(copy(weight.at[a, b], kernels.at[k], w_sem.at[k]))
    copies[0].start()
    if len(sources) > 1:
        load(1, sources[1])
    for c in copies[1:]:
        c.start()
    if stage != "a":
        acc_copies = [copy(acc_in.at[o], acc.at[o], io_sem.at[o, 3]) for o in range(acc.shape[0])]
        for c in acc_copies:
            c.start()

    if stage == "a":
        affine[...] = affine_of(
            scalars, total_ref[...], gain_ref[...], shift_ref[...], cells_per_frame, per_group
        )
        affine_out[...] = affine[...]
    else:
        affine[...] = affine_in[...]

    def params(frame):
        request = scalars[REQ_OF + frame]
        factor = affine[pl.ds(request, 1), :] * 0.5
        term = affine[pl.ds(request + 4, 1), :] * 0.5
        return factor, term

    loaded(0)
    normalize_rows(raw, stacked, 0, range(rows + 2), *params(sources[0]))
    waited = set()
    started = set()
    for step, (o, a, slot) in enumerate(plan):
        ahead = step == 0 and len(sources) > 1
        if ahead:
            loaded(1)
            factor, term = params(sources[1])
        if stage != "a" and o not in started:
            acc_copies[o].wait()
            started.add(o)
        for b in range(3):
            k = blocks.index((a, b))
            if k not in waited:
                copies[k].wait()
                waited.add(k)
            for half in range(2):
                unit = 2 * b + half
                span = slice(half * (channels // 2), (half + 1) * (channels // 2))
                part = jnp.dot(
                    stacked[slot, b : b + rows].reshape(cells, 3 * channels),
                    kernels[k, :, span],
                    preferred_element_type=jnp.float32,
                )
                if o in started or b > 0:
                    acc[o, :, span] += part
                else:
                    acc[o, :, span] = part
                if ahead:
                    turn = range(2 * unit, min(2 * unit + 2, rows + 2))
                    normalize_rows(raw, stacked, 1, turn, factor, term)
        started.add(o)

    def finish(o):
        c = copy(lat.at[o], raw.at[0, pl.ds(1, rows)], io_sem.at[0, 0])
        c.start()
        c.wait()
        for i in range(rows):
            value = raw[0, 1 + i].astype(jnp.float32) + acc[o, i * cols : (i + 1) * cols]
            out_tile[i] = (value + bias_ref[...]).astype(jnp.bfloat16)
        c = copy(out_tile, decoded.at[o], io_sem.at[0, 1])
        c.start()
        c.wait()

    if stage == "a":
        outs = [copy(acc.at[o], acc_out.at[o], io_sem.at[o, 3]) for o in range(2)]
        for c in outs:
            c.start()
        for c in outs:
            c.wait()
    elif stage == "b":
        c = copy(acc.at[0], acc_out.at[0], io_sem.at[0, 3])
        c.start()
        finish(1)
        c.wait()
    else:
        finish(0)


def conv_stage(stage, scalars, latents, extras, weight, small, acc=None, decoded=None, per_group=16, cells_per_frame=0):
    frames, rows, cols, channels = latents.shape
    any_spec = pl.BlockSpec(memory_space=pl.ANY)
    vmem = pl.BlockSpec(memory_space=pltpu.VMEM)
    args = [scalars, latents, *extras, weight, *small]
    specs = [pl.BlockSpec(memory_space=pltpu.SMEM)] + [any_spec] * (2 + len(extras)) + [vmem] * len(small)
    aliases = {}
    if acc is not None:
        args.append(acc)
        specs.append(any_spec)
    acc_shape = lambda n: jax.ShapeDtypeStruct((n, rows * cols, channels), jnp.float32)
    out_shape = jax.ShapeDtypeStruct(latents.shape, jnp.bfloat16)
    if stage == "a":
        outs = (jax.ShapeDtypeStruct((8, channels), jnp.float32), acc_shape(2))
        out_specs = (vmem, any_spec)
        slots, blocks, held = 2, 6, 2
    elif stage == "b":
        outs = (acc_shape(1), out_shape)
        out_specs = (any_spec, any_spec)
        slots, blocks, held = 2, 6, 2
    else:
        aliases = {len(args): 0}
        args.append(decoded)
        specs.append(any_spec)
        outs = out_shape
        out_specs = any_spec
        slots, blocks, held = 1, 3, 1
    return pl.pallas_call(
        functools.partial(conv_kernel, stage, cells_per_frame, per_group),
        in_specs=specs,
        out_specs=out_specs,
        out_shape=outs,
        input_output_aliases=aliases,
        scratch_shapes=[
            pltpu.VMEM((slots, rows + 2, cols, channels), jnp.bfloat16),
            pltpu.VMEM((slots, rows + 2, cols, 3 * channels), jnp.bfloat16),
            pltpu.VMEM((blocks, 3 * channels, channels), jnp.bfloat16),
            pltpu.VMEM((held, rows * cols, channels), jnp.float32),
            pltpu.VMEM((8, channels), jnp.float32),
            pltpu.VMEM((rows, cols, channels), jnp.bfloat16),
            pltpu.SemaphoreType.DMA((2, 4)),
            pltpu.SemaphoreType.DMA((blocks,)),
        ],
        compiler_params=pltpu.CompilerParams(vmem_limit_bytes=56 << 20),
        name="conv_" + stage,
    )(*args)


def pair(axis, partner):
    return [(i, partner(i)) for i in range(lax.axis_size(axis))]


def exchange_sum(value, axis, partner):
    return value + lax.ppermute(value, axis, pair(axis, partner))


def shards(latents, frame_counts, norm_gain, norm_shift, conv_weight, conv_bias):
    frames, rows, cols, channels = latents.shape
    per_group = channels // GROUPS
    spread = ("req", "span")
    request_end = jnp.cumsum(frame_counts)
    request_start = request_end - frame_counts
    first = lax.axis_index(spread) * frames
    tile = lax.axis_index("tile")
    positions = first - 2 + jnp.arange(4, dtype=jnp.int32)
    held = jnp.maximum(positions, 0)
    request = jnp.sum((held[:, None] >= request_end[None, :]).astype(jnp.int32), axis=1)
    start = jnp.sum(
        jnp.where(request[2:, None] == jnp.arange(4)[None, :], request_start[None, :], 0), axis=1
    )
    sources = jnp.maximum(
        positions[2:, None] - 2 + jnp.arange(2, dtype=jnp.int32)[None, :], start[:, None]
    ) - first + 2
    scalars = jnp.concatenate(
        [
            request,
            sources.reshape(-1),
            jnp.stack([tile == 0, tile == lax.axis_size("tile") - 1, tile % 2 == 1]).astype(jnp.int32),
            frame_counts,
        ]
    ).astype(jnp.int32)

    onward = [(i, i + 1) for i in range(lax.axis_size("req") * lax.axis_size("span") - 1)]
    count = lax.axis_size("tile")
    down = [(i, i + 1) for i in range(count - 1)]
    up = [(i + 1, i) for i in range(count - 1)]
    top = lax.ppermute(latents[:, -1], "tile", down)
    bottom = lax.ppermute(latents[:, 0], "tile", up)
    rem = lax.ppermute(latents, spread, onward)
    core = tile % 2
    edge = lax.ppermute(jnp.where(core == 0, top, bottom), spread, onward)
    inner = lax.ppermute(
        jnp.where(core == 0, rem[:, -1], rem[:, 0]), "tile", [(i, i ^ 1) for i in range(count)]
    )

    total = local_stats(scalars, latents, per_group)
    for axis in ("tile", "req", "span"):
        step = 1
        while step < lax.axis_size(axis):
            total = exchange_sum(total, axis, lambda i: i ^ step)
            step *= 2

    cells_per_frame = rows * count * cols * per_group
    weight = conv_weight.reshape(3, 3, 3 * channels, channels)
    gain, shift, bias = (v.reshape(1, channels) for v in (norm_gain, norm_shift, conv_bias))
    run = functools.partial(conv_stage, per_group=per_group, cells_per_frame=cells_per_frame)
    near = (top, bottom)
    far = (top, bottom, rem, edge, inner)
    affine, acc = run("a", scalars, latents, near, weight, (total, gain, shift))
    acc, decoded = run("b", scalars, latents, far, weight, (affine, bias), acc)
    return run("c", scalars, latents, far, weight, (affine, bias), acc, decoded)


def solution(mesh):
    placed = (P(("req", "span"), "tile", None, None), P(), P(), P(), P(), P())
    return jax.shard_map(
        shards,
        mesh=mesh,
        in_specs=placed,
        out_specs=P(("req", "span"), "tile", None, None),
        check_vma=False,
    )
```

time: 288 us -> 147 us (0.51)
  the two profiles are of different devices: /device:TPU:41 before, /device:TPU:0 now
where the time goes in v1:
time: 147 us
  Pallas kernels  57.2 us (39%)
  waiting for transfers between devices  52.6 us (36%)
  starting transfers between devices  26.3 us (18%)
  local copies, waits for them, and re-layouts  6.67 us (5%)
  other arithmetic  3.46 us (2%)
    pallas_call x3, Pallas kernels, conv_stage(): pl.pallas_call(functools.partial(conv_kernel, stage, cells_per_frame, per...  53.6 us
    ppermute x1, waiting for transfers between devices, shards(): rem = lax.ppermute(latents, spread, onward)  36.3 us
    ppermute x7, waiting for transfers between devices, exchange_sum(): return value + lax.ppermute(value, axis, pair(axis, partner))  16 us
    ppermute x7, starting transfers between devices, exchange_sum(): return value + lax.ppermute(value, axis, pair(axis, partner))  15.1 us
    unnamed x11, local copies, waits for them, and re-layouts  3.93 us
    pallas_call x1, Pallas kernels, local_stats(): pl.pallas_call(functools.partial(stats_kernel, per_group), grid_spec=pltp...  3.68 us
    ppermute x1, starting transfers between devices, shards(): rem = lax.ppermute(latents, spread, onward)  3.63 us
    ppermute x1, starting transfers between devices, shards(): edge = lax.ppermute(jnp.where(core == 0, top, bottom), spread, onward)  3.28 us
  transfers between devices with their start and end apart: 12, of which 9 were waited for; matrix products, arithmetic and copies ran while one was open for 4% of the time, Pallas kernels for 18%

profile of v1, /device:TPU:0, one launch (start us, length us, event | category | flops | bytes accessed | tf_op | source)
XLA Modules:
  0.0 146.7 jit_solution(15049121312277640179)
XLA Ops:
  0.0 3.1 %copy.13 = bf16[2,8,128,512]{3,2,0,1:T(8,128)(2,1)} copy(bf16[2,8,128,512]{3,2,1,0:T(8,128)(2,1)} %refs_1_.5) | data formatting | bytes 4194304 | tf_op args[0]
  3.1 3.6 %collective-permute-start.2 = (bf16[2,8,128,512]{3,2,0,1:T(8,128)(2,1)}, bf16[2,8,128,512]{3,2,0,1:T(8,128)(2,1)S(1)}, u32[]{:S(2)}, u32[]{:S(2)}) collective-permute-start(bf16[2,8,128,512]{3,2,0,1:T(8,128)(2,1)} %copy.13), channel_id=1, source_target_pairs={{0,1},{1,2},{2,3},{3,32},{32,33},{33,34},{34,35},{35,64},{64,65},{... | collective-permute-start | bytes 6291464 | tf_op jit(solution)/shard_map/ppermute | solution.py:395
  6.7 1.1 slice_bitcast_fusion
  7.8 1.3 collective-permute-start.1
  9.1 3.0 %collective-permute-start = (bf16[2,128,512]{2,1,0:T(8,128)(2,1)S(1)}, bf16[2,128,512]{2,1,0:T(8,128)(2,1)S(1)}, u32[]{:S(2)}, u32[]{:S(2)}) collective-permute-start(bf16[2,128,512]{2,1,0:T(8,128)(2,1)S(1)} %get-tuple-element.14), channel_id=1, source_target_pairs={{0,4},{4,8},{8,12},{12,16},{16,20},{20,24},{24,28},{1,5},{5,9},{9,... | collective-permute-start | bytes 786440 | tf_op jit(solution)/shard_map/ppermute | solution.py:393
  12.4 0.2 convert_reduce_fusion
  12.9 0.4 collective-permute-done.refs_2_
  13.3 3.3 %collective-permute-start.3 = (bf16[2,128,512]{2,1,0:T(8,128)(2,1)S(1)}, bf16[2,128,512]{2,1,0:T(8,128)(2,1)S(1)}, u32[]{:S(2)}, u32[]{:S(2)}) collective-permute-start(bf16[2,128,512]{2,1,0:T(8,128)(2,1)S(1)} %broadcast_select_fusion), channel_id=1, source_target_pairs={{0,1},{1,2},{2,3},{3,32},{32,33},{33,34},{34,35},{35,64},{64,65},{... | collective-permute-start | bytes 786440 | tf_op jit(solution)/shard_map/ppermute | solution.py:397
  16.6 36.3 %collective-permute-done.2 = bf16[2,8,128,512]{3,2,0,1:T(8,128)(2,1)S(1)} collective-permute-done((bf16[2,8,128,512]{3,2,0,1:T(8,128)(2,1)}, bf16[2,8,128,512]{3,2,0,1:T(8,128)(2,1)S(1)}, u32[]{:S(2)}, u32[]{:S(2)}) %collective-permute-start.2) | collective-permute-done | bytes 2097184 | tf_op jit(solution)/shard_map/ppermute | solution.py:395
  52.9 0.7 fusion
  53.9 0.6 pad_add_fusion.scalars.refs_0_
  54.5 3.7 %local_stats.1 = f32[8,128]{1,0:T(8,128)} custom-call(s32[15]{0:T(128)} %pad_add_fusion.scalars.refs_0_, bf16[2,8,128,512]{3,2,1,0:T(8,128)(2,1)} %refs_1_.5), custom_call_target="tpu_custom_call" | custom-call | tf_op jit(solution)/shard_map/local_stats/pallas_call | solution.py:68
  58.2 0.5 collective-permute-start.5
  58.7 1.0 collective-permute-done.5
  59.8 0.7 add.73
  60.4 1.6 %collective-permute-start.6 = (f32[8,128]{1,0:T(8,128)S(1)}, f32[8,128]{1,0:T(8,128)S(1)}, u32[]{:S(2)}, u32[]{:S(2)}) collective-permute-start(f32[8,128]{1,0:T(8,128)S(1)} %add.73), channel_id=1, source_target_pairs={{0,8},{4,12},{8,0},{12,4},{16,24},{20,28},{24,16},{28,20},{1,9},{5... | collective-permute-start | bytes 12296 | tf_op jit(solution)/shard_map/ppermute | solution.py:360
  62.0 2.0 %collective-permute-done.6 = f32[8,128]{1,0:T(8,128)S(1)} collective-permute-done((f32[8,128]{1,0:T(8,128)S(1)}, f32[8,128]{1,0:T(8,128)S(1)}, u32[]{:S(2)}, u32[]{:S(2)}) %collective-permute-start.6) | collective-permute-done | bytes 4128 | tf_op jit(solution)/shard_map/ppermute | solution.py:360
  64.1 3.2 %collective-permute-start.7 = (f32[8,128]{1,0:T(8,128)S(1)}, f32[8,128]{1,0:T(8,128)S(1)}, u32[]{:S(2)}, u32[]{:S(2)}) collective-permute-start(f32[8,128]{1,0:T(8,128)S(1)} %add.74), channel_id=1, source_target_pairs={{0,16},{4,20},{8,24},{12,28},{16,0},{20,4},{24,8},{28,12},{1,17},{... | collective-permute-start | bytes 12296 | tf_op jit(solution)/shard_map/ppermute | solution.py:360
  67.2 1.9 %collective-permute-done.7 = f32[8,128]{1,0:T(8,128)S(1)} collective-permute-done((f32[8,128]{1,0:T(8,128)S(1)}, f32[8,128]{1,0:T(8,128)S(1)}, u32[]{:S(2)}, u32[]{:S(2)}) %collective-permute-start.7) | collective-permute-done | bytes 4128 | tf_op jit(solution)/shard_map/ppermute | solution.py:360
  69.2 4.9 %collective-permute-start.8 = (f32[8,128]{1,0:T(8,128)S(1)}, f32[8,128]{1,0:T(8,128)S(1)}, u32[]{:S(2)}, u32[]{:S(2)}) collective-permute-start(f32[8,128]{1,0:T(8,128)S(1)} %add.75), channel_id=1, source_target_pairs={{0,32},{32,0},{64,96},{96,64},{1,33},{33,1},{65,97},{97,65},{2,34}... | collective-permute-start | bytes 12296 | tf_op jit(solution)/shard_map/ppermute | solution.py:360
  74.1 1.6 %collective-permute-done.8 = f32[8,128]{1,0:T(8,128)S(1)} collective-permute-done((f32[8,128]{1,0:T(8,128)S(1)}, f32[8,128]{1,0:T(8,128)S(1)}, u32[]{:S(2)}, u32[]{:S(2)}) %collective-permute-start.8) | collective-permute-done | bytes 4128 | tf_op jit(solution)/shard_map/ppermute | solution.py:360
  75.7 4.0 %collective-permute-start.9 = (f32[8,128]{1,0:T(8,128)S(1)}, f32[8,128]{1,0:T(8,128)S(1)}, u32[]{:S(2)}, u32[]{:S(2)}) collective-permute-start(f32[8,128]{1,0:T(8,128)S(1)} %add.76), channel_id=1, source_target_pairs={{0,64},{32,96},{64,0},{96,32},{1,65},{33,97},{65,1},{97,33},{2,66}... | collective-permute-start | bytes 12296 | tf_op jit(solution)/shard_map/ppermute | solution.py:360
  79.7 1.6 %collective-permute-done.9 = f32[8,128]{1,0:T(8,128)S(1)} collective-permute-done((f32[8,128]{1,0:T(8,128)S(1)}, f32[8,128]{1,0:T(8,128)S(1)}, u32[]{:S(2)}, u32[]{:S(2)}) %collective-permute-start.9) | collective-permute-done | bytes 4128 | tf_op jit(solution)/shard_map/ppermute | solution.py:360
  81.2 3.6 %collective-permute-done.10 = f32[8,128]{1,0:T(8,128)S(1)} collective-permute-done((f32[8,128]{1,0:T(8,128)S(1)}, f32[8,128]{1,0:T(8,128)S(1)}, u32[]{:S(2)}, u32[]{:S(2)}) %collective-permute-start.10) | collective-permute-done | bytes 4128 | tf_op jit(solution)/shard_map/ppermute | solution.py:360
  84.9 0.9 collective-permute-start.11
  85.8 4.2 %collective-permute-done.11 = f32[8,128]{1,0:T(8,128)S(1)} collective-permute-done((f32[8,128]{1,0:T(8,128)S(1)}, f32[8,128]{1,0:T(8,128)S(1)}, u32[]{:S(2)}, u32[]{:S(2)}) %collective-permute-start.11) | collective-permute-done | bytes 4128 | tf_op jit(solution)/shard_map/ppermute | solution.py:360
  90.0 0.6 add.79.refs_5_
  90.6 23.1 %conv_a.1 = (f32[8,512]{1,0:T(8,128)}, f32[2,1024,512]{2,1,0:T(8,128)}) custom-call(s32[15]{0:T(128)} %pad_add_fusion.scalars.refs_0_, bf16[2,8,128,512]{3,2,1,0:T(8,128)(2,1)} %refs_1_.5, bf16[2,128,512]{2,1,0:T(8,128)(2,1)} %copy-done.1, bf16[2,128,512]{2,1,0:T(8,128)(2,1)} %copy-done, bf16[3,3,1536,512]{3,2,1,0:T(8,128)(2,1)} %bitcast.16, ...), custom_call_target="tpu_custom_call" | custom-call | tf_op jit(solution)/shard_map/conv_a/pallas_call | solution.py:334
  113.7 1.5 %copy.17.refs_4_ = bf16[2,8,128,512]{3,2,1,0:T(8,128)(2,1)} copy(bf16[2,8,128,512]{3,2,0,1:T(8,128)(2,1)S(1)} %collective-permute-done.2) | data formatting | bytes 4194304 | tf_op jit(solution)/shard_map/ppermute | solution.py:395
  115.2 0.7 copy-done.2
  116.0 19.9 %conv_b.1 = (f32[1,1024,512]{2,1,0:T(8,128)}, bf16[2,8,128,512]{3,2,1,0:T(8,128)(2,1)}) custom-call(s32[15]{0:T(128)} %pad_add_fusion.scalars.refs_0_, bf16[2,8,128,512]{3,2,1,0:T(8,128)(2,1)} %refs_1_.5, bf16[2,128,512]{2,1,0:T(8,128)(2,1)} %copy-done.1, bf16[2,128,512]{2,1,0:T(8,128)(2,1)} %copy-done, bf16[2,8,128,512]{3,2,1,0:T(8,128)(2,1)} %copy.17.refs_4_, ...), custom_call_target="tpu_custom_call" | custom-call | tf_op jit(solution)/shard_map/conv_b/pallas_call | solution.py:334
  135.9 10.6 %conv_c.1 = bf16[2,8,128,512]{3,2,1,0:T(8,128)(2,1)} custom-call(s32[15]{0:T(128)} %pad_add_fusion.scalars.refs_0_, bf16[2,8,128,512]{3,2,1,0:T(8,128)(2,1)} %refs_1_.5, bf16[2,128,512]{2,1,0:T(8,128)(2,1)} %copy-done.1, bf16[2,128,512]{2,1,0:T(8,128)(2,1)} %copy-done, bf16[2,8,128,512]{3,2,1,0:T(8,128)(2,1)} %copy.17.refs_4_, ...), custom_call_target="tpu_custom_call", output_to_operand_aliasing={{}: (11, {})} | custom-call | tf_op jit(solution)/shard_map/conv_c/pallas_call | solution.py:334
  (29 shorter events, 0.9 us)
Async XLA Ops:
  0.0 12.2 %copy-start.4 = (s32[4]{0:T(128)S(1)}, s32[4]{0:T(128)}, u32[]{:S(2)}) copy-start(s32[4]{0:T(128)} %param.7) | copy-start | bytes 52
  3.1 49.8 %collective-permute-start.2 = (bf16[2,8,128,512]{3,2,0,1:T(8,128)(2,1)}, bf16[2,8,128,512]{3,2,0,1:T(8,128)(2,1)S(1)}, u32[]{:S(2)}, u32[]{:S(2)}) collective-permute-start(bf16[2,8,128,512]{3,2,0,1:T(8,128)(2,1)} %copy.13), channel_id=1, source_target_pairs={{0,1},{1,2},{2,3},{3,32},{32,33},{33,34},{34,35},{35,64},{64,65},{... | collective-permute-start | bytes 6291464 | tf_op jit(solution)/shard_map/ppermute | solution.py:395
  7.8 5.1 %collective-permute-start.1 = (bf16[2,128,512]{2,1,0:T(8,128)(2,1)S(1)}, bf16[2,128,512]{2,1,0:T(8,128)(2,1)S(1)}, u32[]{:S(2)}, u32[]{:S(2)}) collective-permute-start(bf16[2,128,512]{2,1,0:T(8,128)(2,1)S(1)} %get-tuple-element.13), channel_id=1, source_target_pairs={{4,0},{8,4},{12,8},{16,12},{20,16},{24,20},{28,24},{5,1},{9,5},{13... | collective-permute-start | bytes 786440 | tf_op jit(solution)/shard_map/ppermute | solution.py:394
  9.1 4.2 %collective-permute-start = (bf16[2,128,512]{2,1,0:T(8,128)(2,1)S(1)}, bf16[2,128,512]{2,1,0:T(8,128)(2,1)S(1)}, u32[]{:S(2)}, u32[]{:S(2)}) collective-permute-start(bf16[2,128,512]{2,1,0:T(8,128)(2,1)S(1)} %get-tuple-element.14), channel_id=1, source_target_pairs={{0,4},{4,8},{8,12},{12,16},{16,20},{20,24},{24,28},{1,5},{5,9},{9,... | collective-permute-start | bytes 786440 | tf_op jit(solution)/shard_map/ppermute | solution.py:393
  12.9 77.6 %copy-start = (bf16[2,128,512]{2,1,0:T(8,128)(2,1)}, bf16[2,128,512]{2,1,0:T(8,128)(2,1)S(1)}, u32[]{:S(2)}) copy-start(bf16[2,128,512]{2,1,0:T(8,128)(2,1)S(1)} %collective-permute-done.1.refs_3_) | copy-start | bytes 786436
  13.3 77.3 %copy-start.1 = (bf16[2,128,512]{2,1,0:T(8,128)(2,1)}, bf16[2,128,512]{2,1,0:T(8,128)(2,1)S(1)}, u32[]{:S(2)}) copy-start(bf16[2,128,512]{2,1,0:T(8,128)(2,1)S(1)} %collective-permute-done.refs_2_) | copy-start | bytes 786436
  13.3 101.9 %collective-permute-start.3 = (bf16[2,128,512]{2,1,0:T(8,128)(2,1)S(1)}, bf16[2,128,512]{2,1,0:T(8,128)(2,1)S(1)}, u32[]{:S(2)}, u32[]{:S(2)}) collective-permute-start(bf16[2,128,512]{2,1,0:T(8,128)(2,1)S(1)} %broadcast_select_fusion), channel_id=1, source_target_pairs={{0,1},{1,2},{2,3},{3,32},{32,33},{33,34},{34,35},{35,64},{64,65},{... | collective-permute-start | bytes 786440 | tf_op jit(solution)/shard_map/ppermute | solution.py:397
  53.7 61.6 %collective-permute-start.4 = (bf16[2,128,512]{2,1,0:T(8,128)(2,1)}, bf16[2,128,512]{2,1,0:T(8,128)(2,1)S(1)}, u32[]{:S(2)}, u32[]{:S(2)}) collective-permute-start(bf16[2,128,512]{2,1,0:T(8,128)(2,1)} %fusion), channel_id=1, source_target_pairs={{0,4},{4,0},{8,12},{12,8},{16,20},{20,16},{24,28},{28,24},{1,5},{5... | collective-permute-start | bytes 786440 | tf_op jit(solution)/shard_map/ppermute | solution.py:398
  58.2 1.5 %collective-permute-start.5 = (f32[8,128]{1,0:T(8,128)}, f32[8,128]{1,0:T(8,128)S(1)}, u32[]{:S(2)}, u32[]{:S(2)}) collective-permute-start(f32[8,128]{1,0:T(8,128)} %local_stats.1), channel_id=1, source_target_pairs={{0,4},{4,0},{8,12},{12,8},{16,20},{20,16},{24,28},{28,24},{1,5},{5... | collective-permute-start | bytes 12296 | tf_op jit(solution)/shard_map/ppermute | solution.py:360
  60.4 3.6 %collective-permute-start.6 = (f32[8,128]{1,0:T(8,128)S(1)}, f32[8,128]{1,0:T(8,128)S(1)}, u32[]{:S(2)}, u32[]{:S(2)}) collective-permute-start(f32[8,128]{1,0:T(8,128)S(1)} %add.73), channel_id=1, source_target_pairs={{0,8},{4,12},{8,0},{12,4},{16,24},{20,28},{24,16},{28,20},{1,9},{5... | collective-permute-start | bytes 12296 | tf_op jit(solution)/shard_map/ppermute | solution.py:360
  64.1 5.1 %collective-permute-start.7 = (f32[8,128]{1,0:T(8,128)S(1)}, f32[8,128]{1,0:T(8,128)S(1)}, u32[]{:S(2)}, u32[]{:S(2)}) collective-permute-start(f32[8,128]{1,0:T(8,128)S(1)} %add.74), channel_id=1, source_target_pairs={{0,16},{4,20},{8,24},{12,28},{16,0},{20,4},{24,8},{28,12},{1,17},{... | collective-permute-start | bytes 12296 | tf_op jit(solution)/shard_map/ppermute | solution.py:360
  69.2 6.5 %collective-permute-start.8 = (f32[8,128]{1,0:T(8,128)S(1)}, f32[8,128]{1,0:T(8,128)S(1)}, u32[]{:S(2)}, u32[]{:S(2)}) collective-permute-start(f32[8,128]{1,0:T(8,128)S(1)} %add.75), channel_id=1, source_target_pairs={{0,32},{32,0},{64,96},{96,64},{1,33},{33,1},{65,97},{97,65},{2,34}... | collective-permute-start | bytes 12296 | tf_op jit(solution)/shard_map/ppermute | solution.py:360
  75.7 5.6 %collective-permute-start.9 = (f32[8,128]{1,0:T(8,128)S(1)}, f32[8,128]{1,0:T(8,128)S(1)}, u32[]{:S(2)}, u32[]{:S(2)}) collective-permute-start(f32[8,128]{1,0:T(8,128)S(1)} %add.76), channel_id=1, source_target_pairs={{0,64},{32,96},{64,0},{96,32},{1,65},{33,97},{65,1},{97,33},{2,66}... | collective-permute-start | bytes 12296 | tf_op jit(solution)/shard_map/ppermute | solution.py:360
  81.2 3.6 %collective-permute-start.10 = (f32[8,128]{1,0:T(8,128)S(1)}, f32[8,128]{1,0:T(8,128)S(1)}, u32[]{:S(2)}, u32[]{:S(2)}) collective-permute-start(f32[8,128]{1,0:T(8,128)S(1)} %add.77), channel_id=1, source_target_pairs={{0,1},{1,0},{2,3},{3,2},{4,5},{5,4},{6,7},{7,6},{8,9},{9,8},{10,11... | collective-permute-start | bytes 12296 | tf_op jit(solution)/shard_map/ppermute | solution.py:360
  84.9 5.1 %collective-permute-start.11 = (f32[8,128]{1,0:T(8,128)S(1)}, f32[8,128]{1,0:T(8,128)S(1)}, u32[]{:S(2)}, u32[]{:S(2)}) collective-permute-start(f32[8,128]{1,0:T(8,128)S(1)} %add.78), channel_id=1, source_target_pairs={{0,2},{1,3},{2,0},{3,1},{4,6},{5,7},{6,4},{7,5},{8,10},{9,11},{10,... | collective-permute-start | bytes 12296 | tf_op jit(solution)/shard_map/ppermute | solution.py:360
  115.2 0.7 copy-start.2
  115.2 0.8 copy-start.3

commit v2 on v1

--- a/solution.py
+++ b/solution.py
@@ -12,13 +12,33 @@
 LANES = 128
 HIGHEST = lax.Precision.HIGHEST
 
-REQ_OF = 0
-SOURCE_0 = 4
-SOURCE_1 = 6
-IS_TOP = 8
-IS_BOTTOM = 9
-CORE = 10
-COUNTS = 11
+
+def layout(counts, place, frames):
+    ends = [counts[0]]
+    for r in range(1, 3):
+        ends.append(ends[-1] + counts[r])
+    first = place[0] * frames
+
+    def request_of(position):
+        request = 0
+        for end in ends:
+            request += (position >= end).astype(jnp.int32)
+        return request
+
+    def start_of(position):
+        start = 0
+        for end in ends:
+            start = jnp.where(position >= end, end, start)
+        return start
+
+    def request(k):
+        return request_of(jnp.maximum(first - 2 + k, 0))
+
+    def source(output, tap):
+        position = first + output
+        return jnp.maximum(position - 2 + tap, start_of(position)) - first + 2
+
+    return request, source
 
 
 def group_matrix(channels, per_group, transpose):
@@ -28,7 +48,7 @@
     return (channel // per_group == lane).astype(jnp.float32)
 
 
-def stats_kernel(per_group, scalars, x_ref, out_ref):
+def stats_kernel(per_group, frames, counts, place, x_ref, out_ref):
     frame = pl.program_id(0)
     rows, cols, channels = x_ref.shape[1:]
 
@@ -49,7 +69,7 @@
         for part in (total, squares)
     ]
     row = lax.broadcasted_iota(jnp.int32, (8, LANES), 0)
-    request = scalars[REQ_OF + 2 + frame]
+    request = layout(counts, place, frames)[0](2 + frame)
     mine = jnp.where(row == request, grouped[0], 0.0) + jnp.where(
         row == request + 4, grouped[1], 0.0
     )
@@ -63,27 +83,27 @@
         out_ref[...] += mine
 
 
-def local_stats(scalars, latents, per_group):
+def local_stats(counts, place, latents, per_group):
     frames, rows, cols, channels = latents.shape
     return pl.pallas_call(
-        functools.partial(stats_kernel, per_group),
+        functools.partial(stats_kernel, per_group, frames),
         grid_spec=pltpu.PrefetchScalarGridSpec(
-            num_scalar_prefetch=1,
+            num_scalar_prefetch=2,
             grid=(frames,),
-            in_specs=[pl.BlockSpec((1, rows, cols, channels), lambda f, s: (f, 0, 0, 0))],
-            out_specs=pl.BlockSpec((8, LANES), lambda f, s: (0, 0)),
+            in_specs=[pl.BlockSpec((1, rows, cols, channels), lambda f, *_: (f, 0, 0, 0))],
+            out_specs=pl.BlockSpec((8, LANES), lambda f, *_: (0, 0)),
         ),
         out_shape=jax.ShapeDtypeStruct((8, LANES), jnp.float32),
         name="local_stats",
-    )(scalars, latents)
-
-
-def affine_of(scalars, total, gain, shift, cells_per_frame, per_group):
+    )(counts, place, latents)
+
+
+def affine_of(counts, total, gain, shift, cells_per_frame, per_group):
     channels = gain.shape[1]
     row = lax.broadcasted_iota(jnp.int32, (4, LANES), 0)
     frames = jnp.zeros((4, LANES), jnp.float32)
     for r in range(4):
-        frames = jnp.where(row == r, scalars[COUNTS + r].astype(jnp.float32), frames)
+        frames = jnp.where(row == r, counts[r].astype(jnp.float32), frames)
     cells = frames * float(cells_per_frame)
     mean = total[0:4] / cells
     scale = lax.rsqrt(total[4:8] / cells - mean * mean + EPSILON)
@@ -114,9 +134,12 @@
 def conv_kernel(stage, cells_per_frame, per_group, *refs):
     refs = list(refs)
     take = lambda n: [refs.pop(0) for _ in range(n)]
-    (scalars,) = take(1)
+    counts, place = take(2)
     lat, top, bottom = take(3)
-    rem, edge, inner = take(3) if stage != "a" else (None, None, None)
+    if stage != "a":
+        near_rows, pair_rows, inner_1 = take(3)
+    if stage == "c":
+        far_rows, inner_0 = take(2)
     (weight,) = take(1)
     if stage == "a":
         total_ref, gain_ref, shift_ref = take(3)
@@ -130,24 +153,26 @@
     raw, stacked, kernels, acc, affine, out_tile, io_sem, w_sem = refs
     rows, cols, channels = lat.shape[1:]
     cells = rows * cols
+    request_of, source_of = layout(counts, place, lat.shape[0])
+    tile = place[1]
 
     if stage == "a":
         sources = [2, 3]
         local_only = True
-        second = scalars[SOURCE_1 + 1] - 2
+        second = source_of(1, 1) - 2
         plan = [(0, 2, 0), (1, 2, 1), (1, 1, second)]
     elif stage == "b":
-        sources = [scalars[SOURCE_0 + 1], scalars[SOURCE_1]]
+        sources = [source_of(0, 1), source_of(1, 0)]
         local_only = False
         plan = [(0, 1, 0), (1, 0, 1)]
     else:
-        sources = [scalars[SOURCE_0]]
+        sources = [source_of(0, 0)]
         local_only = False
         plan = [(0, 0, 0)]
 
-    is_top = scalars[IS_TOP] == 1
-    is_bottom = scalars[IS_BOTTOM] == 1
-    first_core = scalars[CORE] == 0
+    is_top = tile == 0
+    is_bottom = tile == place[2] - 1
+    first_core = lax.rem(tile, 2) == 0
 
     def copy(src, dst, sem):
         return pltpu.make_async_copy(src, dst, sem)
@@ -162,12 +187,13 @@
             no()
 
     def load(slot, frame):
-        main, upper, lower = (raw.at[slot, pl.ds(1, rows)], raw.at[slot, 0], raw.at[slot, rows + 1])
-        sems = (io_sem.at[slot, 0], io_sem.at[slot, 1], io_sem.at[slot, 2])
+        upper, lower = raw.at[slot, 0], raw.at[slot, rows + 1]
+        sems = [io_sem.at[slot, k] for k in range(4)]
 
         def from_local():
             k = frame - 2
-            copy(lat.at[k], main, sems[0]).start()
+            copy(lat.at[k, pl.ds(0, rows - 1)], raw.at[slot, pl.ds(1, rows - 1)], sems[0]).start()
+            copy(lat.at[k, rows - 1], raw.at[slot, rows], sems[3]).start()
             pick(
                 is_top,
                 lambda: copy(lat.at[k, 0], upper, sems[1]).start(),
@@ -180,25 +206,59 @@
             )
 
         def from_remote():
-            copy(rem.at[frame], main, sems[0]).start()
-            pick(
-                is_top,
-                lambda: copy(rem.at[frame, 0], upper, sems[1]).start(),
-                lambda: pick(
-                    first_core,
-                    lambda: copy(edge.at[frame], upper, sems[1]).start(),
-                    lambda: copy(inner.at[frame], upper, sems[1]).start(),
-                ),
-            )
-            pick(
-                is_bottom,
-                lambda: copy(rem.at[frame, rows - 1], lower, sems[2]).start(),
-                lambda: pick(
-                    first_core,
-                    lambda: copy(inner.at[frame], lower, sems[2]).start(),
-                    lambda: copy(edge.at[frame], lower, sems[2]).start(),
-                ),
-            )
+            def frame_one():
+                def first():
+                    copy(near_rows, raw.at[slot, pl.ds(2, rows - 1)], sems[0]).start()
+                    copy(pair_rows.at[1], raw.at[slot, 1], sems[3]).start()
+                    pick(
+                        is_top,
+                        lambda: copy(pair_rows.at[1], upper, sems[1]).start(),
+                        lambda: copy(pair_rows.at[0], upper, sems[1]).start(),
+                    )
+                    copy(inner_1.at[0], lower, sems[2]).start()
+
+                def second():
+                    copy(near_rows, raw.at[slot, pl.ds(1, rows - 1)], sems[0]).start()
+                    copy(pair_rows.at[0], raw.at[slot, rows], sems[3]).start()
+                    pick(
+                        is_bottom,
+                        lambda: copy(pair_rows.at[0], lower, sems[1]).start(),
+                        lambda: copy(pair_rows.at[1], lower, sems[1]).start(),
+                    )
+                    copy(inner_1.at[0], upper, sems[2]).start()
+
+                pick(first_core, first, second)
+
+            def frame_zero():
+                body = far_rows.at[pl.ds(1, rows - 1)]
+                tail = far_rows.at[pl.ds(0, rows - 1)]
+
+                def first():
+                    copy(body, raw.at[slot, pl.ds(1, rows - 1)], sems[0]).start()
+                    copy(pair_rows.at[2], raw.at[slot, rows], sems[3]).start()
+                    pick(
+                        is_top,
+                        lambda: copy(far_rows.at[1], upper, sems[1]).start(),
+                        lambda: copy(far_rows.at[0], upper, sems[1]).start(),
+                    )
+                    copy(inner_0.at[0], lower, sems[2]).start()
+
+                def second():
+                    copy(tail, raw.at[slot, pl.ds(2, rows - 1)], sems[0]).start()
+                    copy(pair_rows.at[2], raw.at[slot, 1], sems[3]).start()
+                    pick(
+                        is_bottom,
+                        lambda: copy(far_rows.at[rows - 2], lower, sems[1]).start(),
+                        lambda: copy(far_rows.at[rows - 1], lower, sems[1]).start(),
+                    )
+                    copy(inner_0.at[0], upper, sems[2]).start()
+
+                pick(first_core, first, second)
+
+            if stage == "b":
+                frame_one()
+            else:
+                pick(frame == 1, frame_one, frame_zero)
 
         if local_only:
             from_local()
@@ -206,10 +266,11 @@
             pick(frame >= 2, from_local, from_remote)
 
     def loaded(slot):
-        main, upper, lower = (raw.at[slot, pl.ds(1, rows)], raw.at[slot, 0], raw.at[slot, rows + 1])
-        copy(lat.at[0], main, io_sem.at[slot, 0]).wait()
-        copy(top.at[0], upper, io_sem.at[slot, 1]).wait()
-        copy(top.at[0], lower, io_sem.at[slot, 2]).wait()
+        copy(
+            lat.at[0, pl.ds(0, rows - 1)], raw.at[slot, pl.ds(1, rows - 1)], io_sem.at[slot, 0]
+        ).wait()
+        for k, place in ((1, 0), (2, rows + 1), (3, rows)):
+            copy(lat.at[0, 0], raw.at[slot, place], io_sem.at[slot, k]).wait()
 
     load(0, sources[0])
     blocks = []
@@ -226,20 +287,20 @@
     for c in copies[1:]:
         c.start()
     if stage != "a":
-        acc_copies = [copy(acc_in.at[o], acc.at[o], io_sem.at[o, 3]) for o in range(acc.shape[0])]
+        acc_copies = [copy(acc_in.at[o], acc.at[o], io_sem.at[o, 4]) for o in range(acc.shape[0])]
         for c in acc_copies:
             c.start()
 
     if stage == "a":
         affine[...] = affine_of(
-            scalars, total_ref[...], gain_ref[...], shift_ref[...], cells_per_frame, per_group
+            counts, total_ref[...], gain_ref[...], shift_ref[...], cells_per_frame, per_group
         )
         affine_out[...] = affine[...]
     else:
         affine[...] = affine_in[...]
 
     def params(frame):
-        request = scalars[REQ_OF + frame]
+        request = request_of(frame)
         factor = affine[pl.ds(request, 1), :] * 0.5
         term = affine[pl.ds(request + 4, 1), :] * 0.5
         return factor, term
@@ -290,13 +351,13 @@
         c.wait()
 
     if stage == "a":
-        outs = [copy(acc.at[o], acc_out.at[o], io_sem.at[o, 3]) for o in range(2)]
+        outs = [copy(acc.at[o], acc_out.at[o], io_sem.at[o, 4]) for o in range(2)]
         for c in outs:
             c.start()
         for c in outs:
             c.wait()
     elif stage == "b":
-        c = copy(acc.at[0], acc_out.at[0], io_sem.at[0, 3])
+        c = copy(acc.at[0], acc_out.at[0], io_sem.at[0, 4])
         c.start()
         finish(1)
         c.wait()
@@ -304,12 +365,12 @@
         finish(0)
 
 
-def conv_stage(stage, scalars, latents, extras, weight, small, acc=None, decoded=None, per_group=16, cells_per_frame=0):
-    frames, rows, cols, channels = latents.shape
+def conv_stage(stage, counts, place, latents, extras, weight, small, acc=None, decoded=None, per_group=16, cells_per_frame=0):
+    _, rows, cols, channels = latents.shape
     any_spec = pl.BlockSpec(memory_space=pl.ANY)
     vmem = pl.BlockSpec(memory_space=pltpu.VMEM)
-    args = [scalars, latents, *extras, weight, *small]
-    specs = [pl.BlockSpec(memory_space=pltpu.SMEM)] + [any_spec] * (2 + len(extras)) + [vmem] * len(small)
+    args = [counts, place, latents, *extras, weight, *small]
+    specs = [pl.BlockSpec(memory_space=pltpu.SMEM)] * 2 + [any_spec] * (2 + len(extras)) + [vmem] * len(small)
     aliases = {}
     if acc is not None:
         args.append(acc)
@@ -344,77 +405,81 @@
             pltpu.VMEM((held, rows * cols, channels), jnp.float32),
             pltpu.VMEM((8, channels), jnp.float32),
             pltpu.VMEM((rows, cols, channels), jnp.bfloat16),
-            pltpu.SemaphoreType.DMA((2, 4)),
+            pltpu.SemaphoreType.DMA((2, 5)),
             pltpu.SemaphoreType.DMA((blocks,)),
         ],
         compiler_params=pltpu.CompilerParams(vmem_limit_bytes=56 << 20),
-        name="conv_" + stage,
     )(*args)
 
 
-def pair(axis, partner):
-    return [(i, partner(i)) for i in range(lax.axis_size(axis))]
-
-
-def exchange_sum(value, axis, partner):
-    return value + lax.ppermute(value, axis, pair(axis, partner))
-
-
 def shards(latents, frame_counts, norm_gain, norm_shift, conv_weight, conv_bias):
-    frames, rows, cols, channels = latents.shape
+    _, rows, cols, channels = latents.shape
     per_group = channels // GROUPS
     spread = ("req", "span")
-    request_end = jnp.cumsum(frame_counts)
-    request_start = request_end - frame_counts
-    first = lax.axis_index(spread) * frames
     tile = lax.axis_index("tile")
-    positions = first - 2 + jnp.arange(4, dtype=jnp.int32)
-    held = jnp.maximum(positions, 0)
-    request = jnp.sum((held[:, None] >= request_end[None, :]).astype(jnp.int32), axis=1)
-    start = jnp.sum(
-        jnp.where(request[2:, None] == jnp.arange(4)[None, :], request_start[None, :], 0), axis=1
-    )
-    sources = jnp.maximum(
-        positions[2:, None] - 2 + jnp.arange(2, dtype=jnp.int32)[None, :], start[:, None]
-    ) - first + 2
-    scalars = jnp.concatenate(
-        [
-            request,
-            sources.reshape(-1),
-            jnp.stack([tile == 0, tile == lax.axis_size("tile") - 1, tile % 2 == 1]).astype(jnp.int32),
-            frame_counts,
-        ]
-    ).astype(jnp.int32)
+    place = jnp.stack([lax.axis_index(spread), tile, lax.axis_size("tile")]).astype(jnp.int32)
 
     onward = [(i, i + 1) for i in range(lax.axis_size("req") * lax.axis_size("span") - 1)]
     count = lax.axis_size("tile")
     down = [(i, i + 1) for i in range(count - 1)]
     up = [(i + 1, i) for i in range(count - 1)]
-    top = lax.ppermute(latents[:, -1], "tile", down)
-    bottom = lax.ppermute(latents[:, 0], "tile", up)
-    rem = lax.ppermute(latents, spread, onward)
+    swap = [(i, i ^ 1) for i in range(count)]
     core = tile % 2
-    edge = lax.ppermute(jnp.where(core == 0, top, bottom), spread, onward)
-    inner = lax.ppermute(
-        jnp.where(core == 0, rem[:, -1], rem[:, 0]), "tile", [(i, i ^ 1) for i in range(count)]
+    first_core = core == 0
+
+    def after(value, *others):
+        return lax.optimization_barrier((value, *others))[0]
+
+    def fold(value, axis, partner):
+        return value + lax.ppermute(value, axis, partner)
+
+    ring = lambda step: [(i, i ^ 1 if step == 0 else 3 - i) for i in range(4)]
+    rung = lambda step: [
+        (i, 2 * (i // 2 ^ 1 if step == 0 else 3 - i // 2) + i % 2) for i in range(count)
+    ]
+
+    near_send = lax.dynamic_slice_in_dim(latents[1], 1 - core, rows - 1, axis=0)
+    near_rows = lax.ppermute(near_send, spread, onward)
+    total = local_stats(frame_counts, place, latents, per_group)
+    total = fold(total, "tile", swap)
+    total = fold(total, "tile", rung(0))
+    total = fold(total, "tile", rung(1))
+    top = lax.ppermute(after(latents[:, -1], total), "tile", down)
+    total = fold(total, "req", ring(0))
+    bottom = lax.ppermute(after(latents[:, 0], total), "tile", up)
+    total = fold(total, "req", ring(1))
+    near_rows, total = lax.optimization_barrier((near_rows, total))
+    inner_send = jnp.where(first_core, near_rows[rows - 2], near_rows[0])[None]
+    inner_1 = lax.ppermute(inner_send, "tile", swap)
+    total = fold(total, "span", ring(0))
+    pair_send = jnp.where(
+        first_core,
+        jnp.stack([top[1], latents[1, 0], latents[0, rows - 1]]),
+        jnp.stack([latents[1, rows - 1], bottom[1], latents[0, 0]]),
     )
-
-    total = local_stats(scalars, latents, per_group)
-    for axis in ("tile", "req", "span"):
-        step = 1
-        while step < lax.axis_size(axis):
-            total = exchange_sum(total, axis, lambda i: i ^ step)
-            step *= 2
+    far_send = jnp.where(
+        first_core,
+        jnp.concatenate([top[:1], latents[0, : rows - 1]]),
+        jnp.concatenate([latents[0, 1:], bottom[:1]]),
+    )
+    pair_send, far_send, total = lax.optimization_barrier((pair_send, far_send, total))
+    other = lax.ppermute(total, "span", ring(1))
+    pair_rows = lax.ppermute(pair_send, spread, onward)
+    far_rows = lax.ppermute(far_send, spread, onward)
+    total = total + other
 
     cells_per_frame = rows * count * cols * per_group
     weight = conv_weight.reshape(3, 3, 3 * channels, channels)
     gain, shift, bias = (v.reshape(1, channels) for v in (norm_gain, norm_shift, conv_bias))
     run = functools.partial(conv_stage, per_group=per_group, cells_per_frame=cells_per_frame)
     near = (top, bottom)
-    far = (top, bottom, rem, edge, inner)
-    affine, acc = run("a", scalars, latents, near, weight, (total, gain, shift))
-    acc, decoded = run("b", scalars, latents, far, weight, (affine, bias), acc)
-    return run("c", scalars, latents, far, weight, (affine, bias), acc, decoded)
+    middle = (top, bottom, near_rows, pair_rows, inner_1)
+    affine, acc = run("a", frame_counts, place, latents, near, weight, (total, gain, shift))
+    pair_rows, acc = lax.optimization_barrier((pair_rows, acc))
+    inner_0 = lax.ppermute(pair_rows[2:3], "tile", swap)
+    acc, decoded = run("b", frame_counts, place, latents, middle[:3] + (pair_rows, inner_1), weight, (affine, bias), acc)
+    far = (top, bottom, near_rows, pair_rows, inner_1, far_rows, inner_0)
+    return run("c", frame_counts, place, latents, far, weight, (affine, bias), acc, decoded)
 
 
 def solution(mesh):

time: 147 us -> 133 us (0.905)
  the two profiles are of different devices: /device:TPU:0 before, /device:TPU:41 now
where the time goes in v2:
time: 133 us; the launch traced here: 131 us
  Pallas kernels  57.7 us (43%)
  waiting for transfers between devices  31.9 us (24%)
  starting transfers between devices  31.1 us (23%)
  local copies, waits for them, and re-layouts  6.72 us (5%)
  other arithmetic  3 us (2%)
    pallas_call x3, Pallas kernels, conv_stage(): pl.pallas_call(functools.partial(conv_kernel, stage, cells_per_frame, per...  53.9 us
    ppermute x1, waiting for transfers between devices, shards(): other = lax.ppermute(total, 'span', ring(1))  23.9 us
    ppermute x6, starting transfers between devices, fold(): return value + lax.ppermute(value, axis, partner)  7.37 us
    ppermute x1, starting transfers between devices, shards(): top = lax.ppermute(after(latents[:, -1], total), 'tile', down)  5.45 us
    ppermute x1, waiting for transfers between devices, shards(): bottom = lax.ppermute(after(latents[:, 0], total), 'tile', up)  5.43 us
    pallas_call x1, Pallas kernels, local_stats(): pl.pallas_call(functools.partial(stats_kernel, per_group, frames), grid_s...  3.83 us
    ppermute x1, starting transfers between devices, shards(): inner_0 = lax.ppermute(pair_rows[2:3], 'tile', swap)  3.63 us
    ppermute x1, starting transfers between devices, shards(): near_rows = lax.ppermute(near_send, spread, onward)  3.11 us
  transfers between devices with their start and end apart: 14, of which 5 were waited for; matrix products, arithmetic and copies ran while one was open for 6% of the time, Pallas kernels for 33%

profile of v2, /device:TPU:41, one launch (start us, length us, event | category | flops | bytes accessed | tf_op | source)
XLA Modules:
  0.0 130.8 jit_solution(12449093636443136039)
XLA Ops:
  0.0 0.7 pad_add_fusion.place.refs_1_
  0.7 3.8 %local_stats.1 = f32[8,128]{1,0:T(8,128)} custom-call(s32[4]{0:T(128)} %refs_0_.5, s32[3]{0:T(128)} %pad_add_fusion.place.refs_1_, bf16[2,8,128,512]{3,2,1,0:T(8,128)(2,1)} %refs_2_.5), custom_call_target="tpu_custom_call" | custom-call | tf_op jit(solution)/shard_map/local_stats/pallas_call | solution.py:88
  4.5 0.7 collective-permute-start
  5.2 1.0 collective-permute-done
  6.2 0.2 collective-permute-start.1
  6.4 1.0 dynamic-slice_bitcast_fusion
  7.4 3.1 %collective-permute-start.6 = (bf16[7,128,512]{2,1,0:T(8,128)(2,1)}, bf16[7,128,512]{2,1,0:T(8,128)(2,1)S(1)}, u32[]{:S(2)}, u32[]{:S(2)}) collective-permute-start(bf16[7,128,512]{2,1,0:T(8,128)(2,1)} %dynamic-slice_bitcast_fusion), channel_id=1, source_target_pairs={{0,1},{1,2},{2,3},{3,32},{32,33},{33,34},{34,35},{35,64},{64,65},{... | collective-permute-start | bytes 2752520 | tf_op jit(solution)/shard_map/ppermute | solution.py:442
  10.5 2.2 %collective-permute-start.2 = (f32[8,128]{1,0:T(8,128)S(1)}, f32[8,128]{1,0:T(8,128)S(1)}, u32[]{:S(2)}, u32[]{:S(2)}) collective-permute-start(f32[8,128]{1,0:T(8,128)S(1)} %add.34), channel_id=1, source_target_pairs={{0,24},{4,28},{8,16},{12,20},{16,8},{20,12},{24,0},{28,4},{1,25},{... | collective-permute-start | bytes 12296 | tf_op jit(solution)/shard_map/ppermute | solution.py:434
  12.7 0.8 slice_bitcast_fusion.2
  13.7 5.5 %collective-permute-start.3 = (bf16[2,128,512]{2,1,0:T(8,128)(2,1)}, bf16[2,128,512]{2,1,0:T(8,128)(2,1)S(1)}, u32[]{:S(2)}, u32[]{:S(2)}) collective-permute-start(bf16[2,128,512]{2,1,0:T(8,128)(2,1)} %get-tuple-element.18), channel_id=1, source_target_pairs={{0,4},{4,8},{8,12},{12,16},{16,20},{20,24},{24,28},{1,5},{5,9},{9,... | collective-permute-start | bytes 786440 | tf_op jit(solution)/shard_map/ppermute | solution.py:447
  19.2 1.4 %slice_bitcast_fusion = (bf16[7,128,512]{2,1,0:T(8,128)(2,1)}, bf16[7,128,512]{2,1,0:T(8,128)(2,1)}) fusion(bf16[2,8,128,512]{3,2,1,0:T(8,128)(2,1)S(1)} %copy-done), kind=kLoop, calls=%fused_computation.1 | loop fusion | bytes 3670016 | tf_op jit(solution)/shard_map/squeeze | solution.py:463
  20.6 3.2 %collective-permute-start.7 = (f32[8,128]{1,0:T(8,128)S(1)}, f32[8,128]{1,0:T(8,128)S(1)}, u32[]{:S(2)}, u32[]{:S(2)}) collective-permute-start(f32[8,128]{1,0:T(8,128)S(1)} %add.36), channel_id=1, source_target_pairs={{0,96},{32,64},{64,32},{96,0},{1,97},{33,65},{65,33},{97,1},{2,98}... | collective-permute-start | bytes 12296 | tf_op jit(solution)/shard_map/ppermute | solution.py:434
  23.8 1.9 %collective-permute-start.5 = (bf16[2,128,512]{2,1,0:T(8,128)(2,1)}, bf16[2,128,512]{2,1,0:T(8,128)(2,1)}, u32[]{:S(2)}, u32[]{:S(2)}) collective-permute-start(bf16[2,128,512]{2,1,0:T(8,128)(2,1)} %get-tuple-element.19), channel_id=1, source_target_pairs={{4,0},{8,4},{12,8},{16,12},{20,16},{24,20},{28,24},{5,1},{9,5},{13... | collective-permute-start | bytes 786440 | tf_op jit(solution)/shard_map/ppermute | solution.py:449
  25.7 0.8 slice_bitcast_fusion.5
  26.6 5.4 %collective-permute-done.5.refs_4_ = bf16[2,128,512]{2,1,0:T(8,128)(2,1)} collective-permute-done((bf16[2,128,512]{2,1,0:T(8,128)(2,1)}, bf16[2,128,512]{2,1,0:T(8,128)(2,1)}, u32[]{:S(2)}, u32[]{:S(2)}) %collective-permute-start.5) | collective-permute-done | bytes 262176 | tf_op jit(solution)/shard_map/ppermute | solution.py:449
  32.0 1.0 fusion
  33.0 1.6 %maximum_select_fusion = bf16[8,128,512]{2,1,0:T(8,128)(2,1)S(1)} fusion(bf16[7,128,512]{2,1,0:T(8,128)(2,1)} %get-tuple-element.32, bf16[1,128,512]{2,1,0:T(8,128)(2,1)S(1)} %get-tuple-element.41, bf16[1,128,512]{2,1,0:T(8,128)(2,1)S(1)} %get-tuple-element.39, bf16[7,128,512]{2,1,0:T(8,128)(2,1)} %get-tuple-element.31, pred[]{:T(512)S(6)} %eq.5), kind=kLoop, calls=%fused_computation | loop fusion | flops 1572864 | bytes 3145729 | tf_op jit(solution)/shard_map/jit(_where)/select_n | solution.py:460
  34.6 1.1 collective-permute-start.8
  35.9 1.3 collective-permute-done.8
  37.2 3.0 %collective-permute-start.12 = (bf16[8,128,512]{2,1,0:T(8,128)(2,1)S(1)}, bf16[8,128,512]{2,1,0:T(8,128)(2,1)S(1)}, u32[]{:S(2)}, u32[]{:S(2)}) collective-permute-start(bf16[8,128,512]{2,1,0:T(8,128)(2,1)S(1)} %maximum_select_fusion), channel_id=1, source_target_pairs={{0,1},{1,2},{2,3},{3,32},{32,33},{33,34},{34,35},{35,64},{64,65},{... | collective-permute-start | bytes 3145736 | tf_op jit(solution)/shard_map/ppermute | solution.py:468
  40.2 3.0 %collective-permute-start.9 = (bf16[3,128,512]{2,1,0:T(8,128)(2,1)S(1)}, bf16[3,128,512]{2,1,0:T(8,128)(2,1)S(1)}, u32[]{:S(2)}, u32[]{:S(2)}) collective-permute-start(bf16[3,128,512]{2,1,0:T(8,128)(2,1)S(1)} %maximum_select_fusion.1), channel_id=1, source_target_pairs={{0,1},{1,2},{2,3},{3,32},{32,33},{33,34},{34,35},{35,64},{64,65},{... | collective-permute-start | bytes 1179656 | tf_op jit(solution)/shard_map/ppermute | solution.py:467
  43.1 1.6 %collective-permute-start.10 = (f32[8,128]{1,0:T(8,128)S(1)}, f32[8,128]{1,0:T(8,128)S(1)}, u32[]{:S(2)}, u32[]{:S(2)}) collective-permute-start(f32[8,128]{1,0:T(8,128)S(1)} %add.40), channel_id=1, source_target_pairs={{0,3},{1,2},{2,1},{3,0},{4,7},{5,6},{6,5},{7,4},{8,11},{9,10},{10,... | collective-permute-start | bytes 12296 | tf_op jit(solution)/shard_map/ppermute | solution.py:466
  44.7 2.1 %collective-permute-start.11 = (bf16[1,128,512]{2,1,0:T(8,128)(2,1)S(1)}, bf16[1,128,512]{2,1,0:T(8,128)(2,1)S(1)}, u32[]{:S(2)}, u32[]{:S(2)}) collective-permute-start(bf16[1,128,512]{2,1,0:T(8,128)(2,1)S(1)} %slice_select_fusion), channel_id=1, source_target_pairs={{0,4},{4,0},{8,12},{12,8},{16,20},{20,16},{24,28},{28,24},{1,5},{5... | collective-permute-start | bytes 393224 | tf_op jit(solution)/shard_map/ppermute | solution.py:453
  46.8 23.9 %collective-permute-done.10 = f32[8,128]{1,0:T(8,128)S(1)} collective-permute-done((f32[8,128]{1,0:T(8,128)S(1)}, f32[8,128]{1,0:T(8,128)S(1)}, u32[]{:S(2)}, u32[]{:S(2)}) %collective-permute-start.10) | collective-permute-done | bytes 4128 | tf_op jit(solution)/shard_map/ppermute | solution.py:466
  70.8 0.6 add.41.refs_6_
  71.4 23.0 %shard_map.64 = (f32[8,512]{1,0:T(8,128)}, f32[2,1024,512]{2,1,0:T(8,128)}) custom-call(s32[4]{0:T(128)} %refs_0_.5, s32[3]{0:T(128)} %pad_add_fusion.place.refs_1_, bf16[2,8,128,512]{3,2,1,0:T(8,128)(2,1)} %refs_2_.5, bf16[2,128,512]{2,1,0:T(8,128)(2,1)} %copy-done.2, bf16[2,128,512]{2,1,0:T(8,128)(2,1)} %collective-permute-done.5.refs_4_, ...), custom_call_target="tpu_custom_call" | custom-call | tf_op jit(solution)/shard_map/pallas_call | solution.py:395
  94.4 3.6 %collective-permute-start.13 = (bf16[1,128,512]{2,1,0:T(8,128)(2,1)S(1)}, bf16[1,128,512]{2,1,0:T(8,128)(2,1)S(1)}, u32[]{:S(2)}, u32[]{:S(2)}) collective-permute-start(bf16[1,128,512]{2,1,0:T(8,128)(2,1)S(1)} %slice.63), channel_id=1, source_target_pairs={{0,4},{4,0},{8,12},{12,8},{16,20},{20,16},{24,28},{28,24},{1,5},{5... | collective-permute-start | bytes 393224 | tf_op jit(solution)/shard_map/ppermute | solution.py:479
  98.1 0.6 copy-done.5
  98.7 20.2 %shard_map.65 = (f32[1,1024,512]{2,1,0:T(8,128)}, bf16[2,8,128,512]{3,2,1,0:T(8,128)(2,1)}) custom-call(s32[4]{0:T(128)} %refs_0_.5, s32[3]{0:T(128)} %pad_add_fusion.place.refs_1_, bf16[2,8,128,512]{3,2,1,0:T(8,128)(2,1)} %refs_2_.5, bf16[2,128,512]{2,1,0:T(8,128)(2,1)} %copy-done.2, bf16[2,128,512]{2,1,0:T(8,128)(2,1)} %collective-permute-done.5.refs_4_, ...), custom_call_target="tpu_custom_call" | custom-call | tf_op jit(solution)/shard_map/pallas_call | solution.py:395
  119.0 0.6 copy-done.9
  119.6 0.4 copy-done.4
  119.9 10.7 %shard_map.66 = bf16[2,8,128,512]{3,2,1,0:T(8,128)(2,1)} custom-call(s32[4]{0:T(128)} %refs_0_.5, s32[3]{0:T(128)} %pad_add_fusion.place.refs_1_, bf16[2,8,128,512]{3,2,1,0:T(8,128)(2,1)} %refs_2_.5, bf16[2,128,512]{2,1,0:T(8,128)(2,1)} %copy-done.2, bf16[2,128,512]{2,1,0:T(8,128)(2,1)} %collective-permute-done.5.refs_4_, ...), custom_call_target="tpu_custom_call", output_to_operand_aliasing={{}: (14, {})} | custom-call | tf_op jit(solution)/shard_map/pallas_call | solution.py:395
  (42 shorter events, 0.4 us)
Async XLA Ops:
  0.7 5.7 %slice-start = ((bf16[2,8,128,512]{3,2,1,0:T(8,128)(2,1)}), bf16[1,8,128,512]{3,2,1,0:T(8,128)(2,1)S(1)}, s32[]{:S(2)}) async-start(bf16[2,8,128,512]{3,2,1,0:T(8,128)(2,1)} %refs_2_.5), calls=%async_computation | async-start | bytes 2097152 | tf_op jit(solution)/shard_map/slice | solution.py:441
  4.5 1.7 %copy-start.10 = (f32[8,128]{1,0:T(8,128)S(1)}, f32[8,128]{1,0:T(8,128)}, u32[]{:S(2)}) copy-start(f32[8,128]{1,0:T(8,128)} %local_stats.1) | copy-start | bytes 12292
  4.5 8.2 %copy-start = (bf16[2,8,128,512]{3,2,1,0:T(8,128)(2,1)S(1)}, bf16[2,8,128,512]{3,2,1,0:T(8,128)(2,1)}, u32[]{:S(2)}) copy-start(bf16[2,8,128,512]{3,2,1,0:T(8,128)(2,1)} %refs_2_.5) | copy-start | bytes 6291460
  4.5 1.7 %collective-permute-start = (f32[8,128]{1,0:T(8,128)}, f32[8,128]{1,0:T(8,128)S(1)}, u32[]{:S(2)}, u32[]{:S(2)}) collective-permute-start(f32[8,128]{1,0:T(8,128)} %local_stats.1), channel_id=1, source_target_pairs={{0,4},{4,0},{8,12},{12,8},{16,20},{20,16},{24,28},{28,24},{1,5},{5... | collective-permute-start | bytes 12296 | tf_op jit(solution)/shard_map/ppermute | solution.py:434
  6.2 4.3 %collective-permute-start.1 = (f32[8,128]{1,0:T(8,128)S(1)}, f32[8,128]{1,0:T(8,128)S(1)}, u32[]{:S(2)}, u32[]{:S(2)}) collective-permute-start(f32[8,128]{1,0:T(8,128)S(1)} %add.33), channel_id=1, source_target_pairs={{0,8},{4,12},{8,0},{12,4},{16,24},{20,28},{24,16},{28,20},{1,9},{5... | collective-permute-start | bytes 12296 | tf_op jit(solution)/shard_map/ppermute | solution.py:434
  7.4 27.2 %collective-permute-start.6 = (bf16[7,128,512]{2,1,0:T(8,128)(2,1)}, bf16[7,128,512]{2,1,0:T(8,128)(2,1)S(1)}, u32[]{:S(2)}, u32[]{:S(2)}) collective-permute-start(bf16[7,128,512]{2,1,0:T(8,128)(2,1)} %dynamic-slice_bitcast_fusion), channel_id=1, source_target_pairs={{0,1},{1,2},{2,3},{3,32},{32,33},{33,34},{34,35},{35,64},{64,65},{... | collective-permute-start | bytes 2752520 | tf_op jit(solution)/shard_map/ppermute | solution.py:442
  10.5 3.2 %collective-permute-start.2 = (f32[8,128]{1,0:T(8,128)S(1)}, f32[8,128]{1,0:T(8,128)S(1)}, u32[]{:S(2)}, u32[]{:S(2)}) collective-permute-start(f32[8,128]{1,0:T(8,128)S(1)} %add.34), channel_id=1, source_target_pairs={{0,24},{4,28},{8,16},{12,20},{16,8},{20,12},{24,0},{28,4},{1,25},{... | collective-permute-start | bytes 12296 | tf_op jit(solution)/shard_map/ppermute | solution.py:434
  13.7 6.9 %collective-permute-start.4 = (f32[8,128]{1,0:T(8,128)S(1)}, f32[8,128]{1,0:T(8,128)S(1)}, u32[]{:S(2)}, u32[]{:S(2)}) collective-permute-start(f32[8,128]{1,0:T(8,128)S(1)} %add.35), channel_id=1, source_target_pairs={{0,32},{32,0},{64,96},{96,64},{1,33},{33,1},{65,97},{97,65},{2,34}... | collective-permute-start | bytes 12296 | tf_op jit(solution)/shard_map/ppermute | solution.py:434
  13.7 12.8 %collective-permute-start.3 = (bf16[2,128,512]{2,1,0:T(8,128)(2,1)}, bf16[2,128,512]{2,1,0:T(8,128)(2,1)S(1)}, u32[]{:S(2)}, u32[]{:S(2)}) collective-permute-start(bf16[2,128,512]{2,1,0:T(8,128)(2,1)} %get-tuple-element.18), channel_id=1, source_target_pairs={{0,4},{4,8},{8,12},{12,16},{16,20},{20,24},{24,28},{1,5},{5,9},{9,... | collective-permute-start | bytes 786440 | tf_op jit(solution)/shard_map/ppermute | solution.py:447
  20.6 5.8 %collective-permute-start.7 = (f32[8,128]{1,0:T(8,128)S(1)}, f32[8,128]{1,0:T(8,128)S(1)}, u32[]{:S(2)}, u32[]{:S(2)}) collective-permute-start(f32[8,128]{1,0:T(8,128)S(1)} %add.36), channel_id=1, source_target_pairs={{0,96},{32,64},{64,32},{96,0},{1,97},{33,65},{65,33},{97,1},{2,98}... | collective-permute-start | bytes 12296 | tf_op jit(solution)/shard_map/ppermute | solution.py:434
  23.8 8.2 %collective-permute-start.5 = (bf16[2,128,512]{2,1,0:T(8,128)(2,1)}, bf16[2,128,512]{2,1,0:T(8,128)(2,1)}, u32[]{:S(2)}, u32[]{:S(2)}) collective-permute-start(bf16[2,128,512]{2,1,0:T(8,128)(2,1)} %get-tuple-element.19), channel_id=1, source_target_pairs={{4,0},{8,4},{12,8},{16,12},{20,16},{24,20},{28,24},{5,1},{9,5},{13... | collective-permute-start | bytes 786440 | tf_op jit(solution)/shard_map/ppermute | solution.py:449
  26.5 9.3 %copy-start.6 = (bf16[1,128,512]{2,1,0:T(8,128)(2,1)S(1)}, bf16[1,128,512]{2,1,0:T(8,128)(2,1)}, u32[]{:S(2)}) copy-start(bf16[1,128,512]{2,1,0:T(8,128)(2,1)} %get-tuple-element.34) | copy-start | bytes 393220
  26.5 9.3 %copy-start.7 = (bf16[1,128,512]{2,1,0:T(8,128)(2,1)S(1)}, bf16[1,128,512]{2,1,0:T(8,128)(2,1)}, u32[]{:S(2)}) copy-start(bf16[1,128,512]{2,1,0:T(8,128)(2,1)} %get-tuple-element.35) | copy-start | bytes 393220
  26.5 9.3 %copy-start.8 = (bf16[1,128,512]{2,1,0:T(8,128)(2,1)S(1)}, bf16[1,128,512]{2,1,0:T(8,128)(2,1)}, u32[]{:S(2)}) copy-start(bf16[1,128,512]{2,1,0:T(8,128)(2,1)} %get-tuple-element.36) | copy-start | bytes 393220
  26.5 8.1 %copy-start.2 = (bf16[2,128,512]{2,1,0:T(8,128)(2,1)}, bf16[2,128,512]{2,1,0:T(8,128)(2,1)S(1)}, u32[]{:S(2)}) copy-start(bf16[2,128,512]{2,1,0:T(8,128)(2,1)S(1)} %collective-permute-done.3.refs_3_) | copy-start | bytes 786436
  34.6 59.7 %copy-start.1 = (bf16[7,128,512]{2,1,0:T(8,128)(2,1)}, bf16[7,128,512]{2,1,0:T(8,128)(2,1)S(1)}, u32[]{:S(2)}) copy-start(bf16[7,128,512]{2,1,0:T(8,128)(2,1)S(1)} %collective-permute-done.6.refs_5_) | copy-start | bytes 2752516
  34.6 2.5 %collective-permute-start.8 = (f32[8,128]{1,0:T(8,128)S(1)}, f32[8,128]{1,0:T(8,128)S(1)}, u32[]{:S(2)}, u32[]{:S(2)}) collective-permute-start(f32[8,128]{1,0:T(8,128)S(1)} %add.39), channel_id=1, source_target_pairs={{0,1},{1,0},{2,3},{3,2},{4,5},{5,4},{6,7},{7,6},{8,9},{9,8},{10,11... | collective-permute-start | bytes 12296 | tf_op jit(solution)/shard_map/ppermute | solution.py:434
  37.2 81.8 %collective-permute-start.12 = (bf16[8,128,512]{2,1,0:T(8,128)(2,1)S(1)}, bf16[8,128,512]{2,1,0:T(8,128)(2,1)S(1)}, u32[]{:S(2)}, u32[]{:S(2)}) collective-permute-start(bf16[8,128,512]{2,1,0:T(8,128)(2,1)S(1)} %maximum_select_fusion), channel_id=1, source_target_pairs={{0,1},{1,2},{2,3},{3,32},{32,33},{33,34},{34,35},{35,64},{64,65},{... | collective-permute-start | bytes 3145736 | tf_op jit(solution)/shard_map/ppermute | solution.py:468
  40.2 54.2 %collective-permute-start.9 = (bf16[3,128,512]{2,1,0:T(8,128)(2,1)S(1)}, bf16[3,128,512]{2,1,0:T(8,128)(2,1)S(1)}, u32[]{:S(2)}, u32[]{:S(2)}) collective-permute-start(bf16[3,128,512]{2,1,0:T(8,128)(2,1)S(1)} %maximum_select_fusion.1), channel_id=1, source_target_pairs={{0,1},{1,2},{2,3},{3,32},{32,33},{33,34},{34,35},{35,64},{64,65},{... | collective-permute-start | bytes 1179656 | tf_op jit(solution)/shard_map/ppermute | solution.py:467
  43.1 27.6 %collective-permute-start.10 = (f32[8,128]{1,0:T(8,128)S(1)}, f32[8,128]{1,0:T(8,128)S(1)}, u32[]{:S(2)}, u32[]{:S(2)}) collective-permute-start(f32[8,128]{1,0:T(8,128)S(1)} %add.40), channel_id=1, source_target_pairs={{0,3},{1,2},{2,1},{3,0},{4,7},{5,6},{6,5},{7,4},{8,11},{9,10},{10,... | collective-permute-start | bytes 12296 | tf_op jit(solution)/shard_map/ppermute | solution.py:466
  44.7 53.3 %collective-permute-start.11 = (bf16[1,128,512]{2,1,0:T(8,128)(2,1)S(1)}, bf16[1,128,512]{2,1,0:T(8,128)(2,1)S(1)}, u32[]{:S(2)}, u32[]{:S(2)}) collective-permute-start(bf16[1,128,512]{2,1,0:T(8,128)(2,1)S(1)} %slice_select_fusion), channel_id=1, source_target_pairs={{0,4},{4,0},{8,12},{12,8},{16,20},{20,16},{24,28},{28,24},{1,5},{5... | collective-permute-start | bytes 393224 | tf_op jit(solution)/shard_map/ppermute | solution.py:453
  94.4 3.7 %copy-start.3 = (bf16[3,128,512]{2,1,0:T(8,128)(2,1)}, bf16[3,128,512]{2,1,0:T(8,128)(2,1)S(1)}, u32[]{:S(2)}) copy-start(bf16[3,128,512]{2,1,0:T(8,128)(2,1)S(1)} %collective-permute-done.9.refs_6_) | copy-start | bytes 1179652
  94.4 24.5 %collective-permute-start.13 = (bf16[1,128,512]{2,1,0:T(8,128)(2,1)S(1)}, bf16[1,128,512]{2,1,0:T(8,128)(2,1)S(1)}, u32[]{:S(2)}, u32[]{:S(2)}) collective-permute-start(bf16[1,128,512]{2,1,0:T(8,128)(2,1)S(1)} %slice.63), channel_id=1, source_target_pairs={{0,4},{4,0},{8,12},{12,8},{16,20},{20,16},{24,28},{28,24},{1,5},{5... | collective-permute-start | bytes 393224 | tf_op jit(solution)/shard_map/ppermute | solution.py:479
  98.1 0.7 copy-start.5
  118.9 0.7 copy-start.9
  119.0 1.0 copy-start.4

commit v3 on v2

--- a/solution.py
+++ b/solution.py
@@ -9,6 +9,7 @@
 
 GROUPS = 32
 EPSILON = 1e-06
+EARLY = 5
 LANES = 128
 HIGHEST = lax.Precision.HIGHEST
 
@@ -120,15 +121,17 @@
 
 def normalize_rows(raw, stacked, slot, rows, factor, term):
     cols, channels = raw.shape[2:]
-    place = lax.broadcasted_iota(jnp.int32, (cols, channels), 0)
+    place = lax.broadcasted_iota(jnp.int32, (cols, LANES), 0)
     for i in rows:
-        u = raw[slot, i].astype(jnp.float32) * factor + term
-        h = u * jnp.tanh(u) + u
-        left = jnp.where(place == 0, h, pltpu.roll(h, 1, 0))
-        right = jnp.where(place == cols - 1, h, pltpu.roll(h, cols - 1, 0))
-        stacked[slot, i, :, 0:channels] = left.astype(jnp.bfloat16)
-        stacked[slot, i, :, channels : 2 * channels] = h.astype(jnp.bfloat16)
-        stacked[slot, i, :, 2 * channels :] = right.astype(jnp.bfloat16)
+        for at in range(0, channels, LANES):
+            lanes = slice(at, at + LANES)
+            u = raw[slot, i, :, lanes].astype(jnp.float32) * factor[:, lanes] + term[:, lanes]
+            h = u * jnp.tanh(u) + u
+            left = jnp.where(place == 0, h, pltpu.roll(h, 1, 0))
+            right = jnp.where(place == cols - 1, h, pltpu.roll(h, cols - 1, 0))
+            for tap, value in enumerate((left, h, right)):
+                begin = tap * channels + at
+                stacked[slot, i, :, begin : begin + LANES] = value.astype(jnp.bfloat16)
 
 
 def conv_kernel(stage, cells_per_frame, per_group, *refs):
@@ -150,7 +153,7 @@
     else:
         affine_in, bias_ref, acc_in, _ = take(4)
         (decoded,) = take(1)
-    raw, stacked, kernels, acc, affine, out_tile, io_sem, w_sem = refs
+    raw, stacked, kernels, acc, affine, held, residual, io_sem, w_sem, out_sem = refs
     rows, cols, channels = lat.shape[1:]
     cells = rows * cols
     request_of, source_of = layout(counts, place, lat.shape[0])
@@ -162,9 +165,9 @@
         second = source_of(1, 1) - 2
         plan = [(0, 2, 0), (1, 2, 1), (1, 1, second)]
     elif stage == "b":
-        sources = [source_of(0, 1), source_of(1, 0)]
+        sources = [source_of(1, 0), source_of(0, 1)]
         local_only = False
-        plan = [(0, 1, 0), (1, 0, 1)]
+        plan = [(1, 0, 0), (0, 1, 1)]
     else:
         sources = [source_of(0, 0)]
         local_only = False
@@ -206,9 +209,15 @@
             )
 
         def from_remote():
+            early = near_rows.shape[0]
+            late = rows - early
+
             def frame_one():
                 def first():
-                    copy(near_rows, raw.at[slot, pl.ds(2, rows - 1)], sems[0]).start()
+                    copy(near_rows, raw.at[slot, pl.ds(late + 1, early)], sems[0]).start()
+                    copy(
+                        pair_rows.at[pl.ds(2, late - 1)], raw.at[slot, pl.ds(2, late - 1)], sems[0]
+                    ).start()
                     copy(pair_rows.at[1], raw.at[slot, 1], sems[3]).start()
                     pick(
                         is_top,
@@ -218,38 +227,40 @@
                     copy(inner_1.at[0], lower, sems[2]).start()
 
                 def second():
-                    copy(near_rows, raw.at[slot, pl.ds(1, rows - 1)], sems[0]).start()
-                    copy(pair_rows.at[0], raw.at[slot, rows], sems[3]).start()
+                    copy(near_rows, raw.at[slot, pl.ds(1, early)], sems[0]).start()
+                    copy(
+                        pair_rows.at[pl.ds(0, late - 1)],
+                        raw.at[slot, pl.ds(early + 1, late - 1)],
+                        sems[0],
+                    ).start()
+                    copy(pair_rows.at[late - 1], raw.at[slot, rows], sems[3]).start()
                     pick(
                         is_bottom,
-                        lambda: copy(pair_rows.at[0], lower, sems[1]).start(),
-                        lambda: copy(pair_rows.at[1], lower, sems[1]).start(),
+                        lambda: copy(pair_rows.at[late - 1], lower, sems[1]).start(),
+                        lambda: copy(pair_rows.at[late], lower, sems[1]).start(),
                     )
                     copy(inner_1.at[0], upper, sems[2]).start()
 
                 pick(first_core, first, second)
 
             def frame_zero():
-                body = far_rows.at[pl.ds(1, rows - 1)]
-                tail = far_rows.at[pl.ds(0, rows - 1)]
-
                 def first():
-                    copy(body, raw.at[slot, pl.ds(1, rows - 1)], sems[0]).start()
-                    copy(pair_rows.at[2], raw.at[slot, rows], sems[3]).start()
+                    copy(far_rows, raw.at[slot, pl.ds(1, rows - 1)], sems[0]).start()
+                    copy(pair_rows.at[late + 2], raw.at[slot, rows], sems[3]).start()
                     pick(
                         is_top,
-                        lambda: copy(far_rows.at[1], upper, sems[1]).start(),
                         lambda: copy(far_rows.at[0], upper, sems[1]).start(),
+                        lambda: copy(pair_rows.at[late + 1], upper, sems[1]).start(),
                     )
                     copy(inner_0.at[0], lower, sems[2]).start()
 
                 def second():
-                    copy(tail, raw.at[slot, pl.ds(2, rows - 1)], sems[0]).start()
-                    copy(pair_rows.at[2], raw.at[slot, 1], sems[3]).start()
+                    copy(far_rows, raw.at[slot, pl.ds(2, rows - 1)], sems[0]).start()
+                    copy(pair_rows.at[late + 2], raw.at[slot, 1], sems[3]).start()
                     pick(
                         is_bottom,
                         lambda: copy(far_rows.at[rows - 2], lower, sems[1]).start(),
-                        lambda: copy(far_rows.at[rows - 1], lower, sems[1]).start(),
+                        lambda: copy(pair_rows.at[late + 1], lower, sems[1]).start(),
                     )
                     copy(inner_0.at[0], upper, sems[2]).start()
 
@@ -272,25 +283,27 @@
         for k, place in ((1, 0), (2, rows + 1), (3, rows)):
             copy(lat.at[0, 0], raw.at[slot, place], io_sem.at[slot, k]).wait()
 
+    half_width = channels // 2
+    pieces, order = [], []
+    for o, a, slot in plan:
+        for b in range(3):
+            order += [(o, a, slot, half, b) for half in range(2)]
+            if (a, b) not in pieces:
+                pieces.append((a, b))
+    loads = [
+        copy(weight.at[a, b], kernels.at[k], w_sem.at[k])
+        for k, (a, b) in enumerate(pieces)
+    ]
+    sent = 0
+
+    def send_until(n):
+        nonlocal sent
+        while sent < min(n, len(loads)):
+            loads[sent].start()
+            sent += 1
+
     load(0, sources[0])
-    blocks = []
-    for _, a, _ in plan:
-        for b in range(3):
-            if (a, b) not in blocks:
-                blocks.append((a, b))
-    copies = []
-    for k, (a, b) in enumerate(blocks):
-        copies.append(copy(weight.at[a, b], kernels.at[k], w_sem.at[k]))
-    copies[0].start()
-    if len(sources) > 1:
-        load(1, sources[1])
-    for c in copies[1:]:
-        c.start()
-    if stage != "a":
-        acc_copies = [copy(acc_in.at[o], acc.at[o], io_sem.at[o, 4]) for o in range(acc.shape[0])]
-        for c in acc_copies:
-            c.start()
-
+    send_until(1)
     if stage == "a":
         affine[...] = affine_of(
             counts, total_ref[...], gain_ref[...], shift_ref[...], cells_per_frame, per_group
@@ -306,63 +319,70 @@
         return factor, term
 
     loaded(0)
+    if len(sources) > 1:
+        load(1, sources[1])
+    send_until(2)
     normalize_rows(raw, stacked, 0, range(rows + 2), *params(sources[0]))
+
+    def held_copy(o):
+        return copy(acc_in.at[o], held.at[o], io_sem.at[o, 4])
+
+    def finish(o):
+        for i in range(rows):
+            for half in range(2):
+                span = slice(half * half_width, (half + 1) * half_width)
+                value = residual[i, :, span].astype(jnp.float32) + (
+                    acc[o, half, i * cols : (i + 1) * cols] + bias_ref[:, span]
+                )
+                residual[i, :, span] = value.astype(jnp.bfloat16)
+            sends.append(copy(residual.at[i], decoded.at[o, i], out_sem.at[i]))
+            sends[-1].start()
+
+    sends = []
     waited = set()
-    started = set()
-    for step, (o, a, slot) in enumerate(plan):
-        ahead = step == 0 and len(sources) > 1
-        if ahead:
+    seen = set()
+    for step, (o, a, slot, half, b) in enumerate(order):
+        ahead = step < 6 and len(sources) > 1
+        if step == 0 and ahead:
             loaded(1)
             factor, term = params(sources[1])
-        if stage != "a" and o not in started:
-            acc_copies[o].wait()
-            started.add(o)
-        for b in range(3):
-            k = blocks.index((a, b))
-            if k not in waited:
-                copies[k].wait()
-                waited.add(k)
-            for half in range(2):
-                unit = 2 * b + half
-                span = slice(half * (channels // 2), (half + 1) * (channels // 2))
-                part = jnp.dot(
-                    stacked[slot, b : b + rows].reshape(cells, 3 * channels),
-                    kernels[k, :, span],
-                    preferred_element_type=jnp.float32,
-                )
-                if o in started or b > 0:
-                    acc[o, :, span] += part
-                else:
-                    acc[o, :, span] = part
-                if ahead:
-                    turn = range(2 * unit, min(2 * unit + 2, rows + 2))
-                    normalize_rows(raw, stacked, 1, turn, factor, term)
-        started.add(o)
-
-    def finish(o):
-        c = copy(lat.at[o], raw.at[0, pl.ds(1, rows)], io_sem.at[0, 0])
-        c.start()
+        k = pieces.index((a, b))
+        if k not in waited:
+            loads[k].wait()
+            waited.add(k)
+            send_until(k + 3)
+        if step == 1 and stage != "a":
+            for n in {o for o, *_ in plan}:
+                held_copy(n).start()
+            copy(lat.at[1 if stage == "b" else 0], residual, out_sem.at[rows]).start()
+        if step == 3 and stage != "a":
+            copy(lat.at[0], residual, out_sem.at[rows]).wait()
+        part = jnp.dot(
+            stacked[slot, b : b + rows].reshape(cells, 3 * channels),
+            kernels[k, :, half * half_width : (half + 1) * half_width],
+            preferred_element_type=jnp.float32,
+        )
+        if stage != "a" and b == 2:
+            if half == 0:
+                held_copy(o).wait()
+            part = part + held[o, half]
+        if (o, half) in seen:
+            acc[o, half] += part
+        else:
+            acc[o, half] = part
+            seen.add((o, half))
+        if ahead:
+            turn = range(2 * step, min(2 * step + 2, rows + 2))
+            normalize_rows(raw, stacked, 1, turn, factor, term)
+        last = not any(x[0] == o and x[3] == half for x in order[step + 1 :])
+        if last and (stage == "c" or (stage == "b" and o == 1)):
+            if half == 1:
+                finish(o)
+        elif last:
+            sends.append(copy(acc.at[o, half], acc_out.at[o, half], io_sem.at[half, 5 + o]))
+            sends[-1].start()
+    for c in sends:
         c.wait()
-        for i in range(rows):
-            value = raw[0, 1 + i].astype(jnp.float32) + acc[o, i * cols : (i + 1) * cols]
-            out_tile[i] = (value + bias_ref[...]).astype(jnp.bfloat16)
-        c = copy(out_tile, decoded.at[o], io_sem.at[0, 1])
-        c.start()
-        c.wait()
-
-    if stage == "a":
-        outs = [copy(acc.at[o], acc_out.at[o], io_sem.at[o, 4]) for o in range(2)]
-        for c in outs:
-            c.start()
-        for c in outs:
-            c.wait()
-    elif stage == "b":
-        c = copy(acc.at[0], acc_out.at[0], io_sem.at[0, 4])
-        c.start()
-        finish(1)
-        c.wait()
-    else:
-        finish(0)
 
 
 def conv_stage(stage, counts, place, latents, extras, weight, small, acc=None, decoded=None, per_group=16, cells_per_frame=0):
@@ -375,7 +395,7 @@
     if acc is not None:
         args.append(acc)
         specs.append(any_spec)
-    acc_shape = lambda n: jax.ShapeDtypeStruct((n, rows * cols, channels), jnp.float32)
+    acc_shape = lambda n: jax.ShapeDtypeStruct((n, 2, rows * cols, channels // 2), jnp.float32)
     out_shape = jax.ShapeDtypeStruct(latents.shape, jnp.bfloat16)
     if stage == "a":
         outs = (jax.ShapeDtypeStruct((8, channels), jnp.float32), acc_shape(2))
@@ -402,13 +422,15 @@
             pltpu.VMEM((slots, rows + 2, cols, channels), jnp.bfloat16),
             pltpu.VMEM((slots, rows + 2, cols, 3 * channels), jnp.bfloat16),
             pltpu.VMEM((blocks, 3 * channels, channels), jnp.bfloat16),
-            pltpu.VMEM((held, rows * cols, channels), jnp.float32),
+            pltpu.VMEM((held, 2, rows * cols, channels // 2), jnp.float32),
             pltpu.VMEM((8, channels), jnp.float32),
+            pltpu.VMEM((held, 2, rows * cols, channels // 2), jnp.float32),
             pltpu.VMEM((rows, cols, channels), jnp.bfloat16),
-            pltpu.SemaphoreType.DMA((2, 5)),
+            pltpu.SemaphoreType.DMA((2, 7)),
             pltpu.SemaphoreType.DMA((blocks,)),
+            pltpu.SemaphoreType.DMA((rows + 1,)),
         ],
-        compiler_params=pltpu.CompilerParams(vmem_limit_bytes=56 << 20),
+        compiler_params=pltpu.CompilerParams(vmem_limit_bytes=58 << 20),
     )(*args)
 
 
@@ -438,7 +460,8 @@
         (i, 2 * (i // 2 ^ 1 if step == 0 else 3 - i // 2) + i % 2) for i in range(count)
     ]
 
-    near_send = lax.dynamic_slice_in_dim(latents[1], 1 - core, rows - 1, axis=0)
+    late = rows - EARLY
+    near_send = lax.dynamic_slice_in_dim(latents[1], late * (1 - core), EARLY, axis=0)
     near_rows = lax.ppermute(near_send, spread, onward)
     total = local_stats(frame_counts, place, latents, per_group)
     total = fold(total, "tile", swap)
@@ -448,21 +471,16 @@
     total = fold(total, "req", ring(0))
     bottom = lax.ppermute(after(latents[:, 0], total), "tile", up)
     total = fold(total, "req", ring(1))
-    near_rows, total = lax.optimization_barrier((near_rows, total))
-    inner_send = jnp.where(first_core, near_rows[rows - 2], near_rows[0])[None]
-    inner_1 = lax.ppermute(inner_send, "tile", swap)
     total = fold(total, "span", ring(0))
     pair_send = jnp.where(
         first_core,
-        jnp.stack([top[1], latents[1, 0], latents[0, rows - 1]]),
-        jnp.stack([latents[1, rows - 1], bottom[1], latents[0, 0]]),
+        jnp.concatenate([top[1:], latents[1, :late], top[:1], latents[0, rows - 1 :]]),
+        jnp.concatenate([latents[1, EARLY:], bottom[1:], bottom[:1], latents[0, :1]]),
     )
-    far_send = jnp.where(
-        first_core,
-        jnp.concatenate([top[:1], latents[0, : rows - 1]]),
-        jnp.concatenate([latents[0, 1:], bottom[:1]]),
-    )
-    pair_send, far_send, total = lax.optimization_barrier((pair_send, far_send, total))
+    far_send = lax.dynamic_slice_in_dim(latents[0], core, rows - 1, axis=0)
+    near_rows, total = lax.optimization_barrier((near_rows, total))
+    inner_send = jnp.where(first_core, near_rows[EARLY - 1], near_rows[0])[None]
+    inner_1 = lax.ppermute(inner_send, "tile", swap)
     other = lax.ppermute(total, "span", ring(1))
     pair_rows = lax.ppermute(pair_send, spread, onward)
     far_rows = lax.ppermute(far_send, spread, onward)
@@ -476,7 +494,7 @@
     middle = (top, bottom, near_rows, pair_rows, inner_1)
     affine, acc = run("a", frame_counts, place, latents, near, weight, (total, gain, shift))
     pair_rows, acc = lax.optimization_barrier((pair_rows, acc))
-    inner_0 = lax.ppermute(pair_rows[2:3], "tile", swap)
+    inner_0 = lax.ppermute(pair_rows[late + 2 :], "tile", swap)
     acc, decoded = run("b", frame_counts, place, latents, middle[:3] + (pair_rows, inner_1), weight, (affine, bias), acc)
     far = (top, bottom, near_rows, pair_rows, inner_1, far_rows, inner_0)
     return run("c", frame_counts, place, latents, far, weight, (affine, bias), acc, decoded)

time: 133 us -> 131 us (0.985)
  the two profiles are of different devices: /device:TPU:41 before, /device:TPU:23 now
where the time goes in v3:
time: 131 us; the launch traced here: 130 us
  Pallas kernels  55 us (42%)
  waiting for transfers between devices  44.5 us (34%)
  starting transfers between devices  20.6 us (16%)
  local copies, waits for them, and re-layouts  6.81 us (5%)
  other arithmetic  2.66 us (2%)
    pallas_call x3, Pallas kernels, conv_stage(): pl.pallas_call(functools.partial(conv_kernel, stage, cells_per_frame, per...  51.1 us
    ppermute x6, waiting for transfers between devices, fold(): return value + lax.ppermute(value, axis, partner)  34.9 us
    ppermute x1, starting transfers between devices, shards(): top = lax.ppermute(after(latents[:, -1], total), 'tile', down)  5.28 us
    ppermute x1, waiting for transfers between devices, shards(): bottom = lax.ppermute(after(latents[:, 0], total), 'tile', up)  5.23 us
    ppermute x6, starting transfers between devices, fold(): return value + lax.ppermute(value, axis, partner)  4.53 us
    pallas_call x1, Pallas kernels, local_stats(): pl.pallas_call(functools.partial(stats_kernel, per_group, frames), grid_s...  3.82 us
    ppermute x1, waiting for transfers between devices, shards(): other = lax.ppermute(total, 'span', ring(1))  3.68 us
    ppermute x1, starting transfers between devices, shards(): near_rows = lax.ppermute(near_send, spread, onward)  3.45 us
  transfers between devices with their start and end apart: 14, of which 6 were waited for; matrix products, arithmetic and copies ran while one was open for 6% of the time, Pallas kernels for 31%

profile of v3, /device:TPU:23, one launch (start us, length us, event | category | flops | bytes accessed | tf_op | source)
XLA Modules:
  0.0 130.0 jit_solution(5946921305827290277)
XLA Ops:
  0.0 0.6 pad_add_fusion.place.refs_1_
  0.6 3.8 %local_stats.1 = f32[8,128]{1,0:T(8,128)} custom-call(s32[4]{0:T(128)} %refs_0_.5, s32[3]{0:T(128)} %pad_add_fusion.place.refs_1_, bf16[2,8,128,512]{3,2,1,0:T(8,128)(2,1)} %refs_2_.5), custom_call_target="tpu_custom_call" | custom-call | tf_op jit(solution)/shard_map/local_stats/pallas_call | solution.py:89
  4.4 0.7 collective-permute-start
  5.1 1.2 fusion
  6.3 1.1 collective-permute-start.1
  7.4 0.9 dynamic-slice_bitcast_fusion.1
  8.3 3.4 %collective-permute-start.6 = (bf16[5,128,512]{2,1,0:T(8,128)(2,1)}, bf16[5,128,512]{2,1,0:T(8,128)(2,1)S(1)}, u32[]{:S(2)}, u32[]{:S(2)}) collective-permute-start(bf16[5,128,512]{2,1,0:T(8,128)(2,1)} %dynamic-slice_bitcast_fusion.1), channel_id=1, source_target_pairs={{0,1},{1,2},{2,3},{3,32},{32,33},{33,34},{34,35},{35,64},{64,65},{... | collective-permute-start | bytes 1966088 | tf_op jit(solution)/shard_map/ppermute | solution.py:465
  11.8 0.8 slice_bitcast_fusion.2
  12.7 1.9 %collective-permute-done.2 = f32[8,128]{1,0:T(8,128)S(1)} collective-permute-done((f32[8,128]{1,0:T(8,128)S(1)}, f32[8,128]{1,0:T(8,128)S(1)}, u32[]{:S(2)}, u32[]{:S(2)}) %collective-permute-start.2) | collective-permute-done | bytes 4128 | tf_op jit(solution)/shard_map/ppermute | solution.py:456
  14.6 1.6 %collective-permute-start.4 = (f32[8,128]{1,0:T(8,128)S(1)}, f32[8,128]{1,0:T(8,128)S(1)}, u32[]{:S(2)}, u32[]{:S(2)}) collective-permute-start(f32[8,128]{1,0:T(8,128)S(1)} %add.37), channel_id=1, source_target_pairs={{0,32},{32,0},{64,96},{96,64},{1,33},{33,1},{65,97},{97,65},{2,34}... | collective-permute-start | bytes 12296 | tf_op jit(solution)/shard_map/ppermute | solution.py:456
  16.2 5.3 %collective-permute-start.3 = (bf16[2,128,512]{2,1,0:T(8,128)(2,1)}, bf16[2,128,512]{2,1,0:T(8,128)(2,1)S(1)}, u32[]{:S(2)}, u32[]{:S(2)}) collective-permute-start(bf16[2,128,512]{2,1,0:T(8,128)(2,1)} %get-tuple-element.15), channel_id=1, source_target_pairs={{0,4},{4,8},{8,12},{12,16},{16,20},{20,24},{24,28},{1,5},{5,9},{9,... | collective-permute-start | bytes 786440 | tf_op jit(solution)/shard_map/ppermute | solution.py:470
  21.5 1.0 slice_bitcast_fusion
  22.5 1.9 %collective-permute-start.5 = (bf16[2,128,512]{2,1,0:T(8,128)(2,1)}, bf16[2,128,512]{2,1,0:T(8,128)(2,1)S(1)}, u32[]{:S(2)}, u32[]{:S(2)}) collective-permute-start(bf16[2,128,512]{2,1,0:T(8,128)(2,1)} %get-tuple-element.16), channel_id=1, source_target_pairs={{4,0},{8,4},{12,8},{16,12},{20,16},{24,20},{28,24},{5,1},{9,5},{13... | collective-permute-start | bytes 786440 | tf_op jit(solution)/shard_map/ppermute | solution.py:472
  24.4 0.7 collective-permute-done.3.refs_3_
  25.1 5.2 %collective-permute-done.5.refs_4_ = bf16[2,128,512]{2,1,0:T(8,128)(2,1)S(1)} collective-permute-done((bf16[2,128,512]{2,1,0:T(8,128)(2,1)}, bf16[2,128,512]{2,1,0:T(8,128)(2,1)S(1)}, u32[]{:S(2)}, u32[]{:S(2)}) %collective-permute-start.5) | collective-permute-done | bytes 262176 | tf_op jit(solution)/shard_map/ppermute | solution.py:472
  30.4 1.4 %maximum_select_fusion = bf16[6,128,512]{2,1,0:T(8,128)(2,1)S(1)} fusion(bf16[1,128,512]{2,1,0:T(8,128)(2,1)S(1)} %get-tuple-element.30, bf16[1,128,512]{2,1,0:T(8,128)(2,1)S(1)} %get-tuple-element.36, bf16[3,128,512]{2,1,0:T(8,128)(2,1)} %get-tuple-element.28, bf16[1,128,512]{2,1,0:T(8,128)(2,1)S(1)} %get-tuple-element.35, ...), kind=kLoop, calls=%fused_computation.1 | loop fusion | flops 2752512 | bytes 2359297 | tf_op jit(solution)/shard_map/jit(_where)/select_n | solution.py:475
  31.8 1.9 %collective-permute-start.9 = (bf16[6,128,512]{2,1,0:T(8,128)(2,1)S(1)}, bf16[6,128,512]{2,1,0:T(8,128)(2,1)S(1)}, u32[]{:S(2)}, u32[]{:S(2)}) collective-permute-start(bf16[6,128,512]{2,1,0:T(8,128)(2,1)S(1)} %maximum_select_fusion), channel_id=1, source_target_pairs={{0,1},{1,2},{2,3},{3,32},{32,33},{33,34},{34,35},{35,64},{64,65},{... | collective-permute-start | bytes 2359304 | tf_op jit(solution)/shard_map/ppermute | solution.py:485
  33.7 1.3 dynamic-slice_bitcast_fusion
  35.0 2.5 %collective-permute-start.12 = (bf16[7,128,512]{2,1,0:T(8,128)(2,1)S(1)}, bf16[7,128,512]{2,1,0:T(8,128)(2,1)S(1)}, u32[]{:S(2)}, u32[]{:S(2)}) collective-permute-start(bf16[7,128,512]{2,1,0:T(8,128)(2,1)S(1)} %dynamic-slice_bitcast_fusion), channel_id=1, source_target_pairs={{0,1},{1,2},{2,3},{3,32},{32,33},{33,34},{34,35},{35,64},{64,65},{... | collective-permute-start | bytes 2752520 | tf_op jit(solution)/shard_map/ppermute | solution.py:486
  37.5 0.2 collective-permute-start.7
  37.7 3.6 %collective-permute-done.7 = f32[8,128]{1,0:T(8,128)S(1)} collective-permute-done((f32[8,128]{1,0:T(8,128)S(1)}, f32[8,128]{1,0:T(8,128)S(1)}, u32[]{:S(2)}, u32[]{:S(2)}) %collective-permute-start.7) | collective-permute-done | bytes 4128 | tf_op jit(solution)/shard_map/ppermute | solution.py:456
  41.3 0.9 collective-permute-start.8
  42.2 29.4 %collective-permute-done.8 = f32[8,128]{1,0:T(8,128)S(1)} collective-permute-done((f32[8,128]{1,0:T(8,128)S(1)}, f32[8,128]{1,0:T(8,128)S(1)}, u32[]{:S(2)}, u32[]{:S(2)}) %collective-permute-start.8) | collective-permute-done | bytes 4128 | tf_op jit(solution)/shard_map/ppermute | solution.py:456
  71.7 0.3 collective-permute-start.11
  72.0 3.7 %collective-permute-done.10 = f32[8,128]{1,0:T(8,128)S(1)} collective-permute-done((f32[8,128]{1,0:T(8,128)S(1)}, f32[8,128]{1,0:T(8,128)S(1)}, u32[]{:S(2)}, u32[]{:S(2)}) %collective-permute-start.10) | collective-permute-done | bytes 4128 | tf_op jit(solution)/shard_map/ppermute | solution.py:484
  75.6 0.6 add.43.refs_6_
  76.2 21.6 %shard_map.64 = (f32[8,512]{1,0:T(8,128)}, f32[2,2,1024,256]{3,2,1,0:T(8,128)}) custom-call(s32[4]{0:T(128)} %refs_0_.5, s32[3]{0:T(128)} %pad_add_fusion.place.refs_1_, bf16[2,8,128,512]{3,2,1,0:T(8,128)(2,1)} %refs_2_.5, bf16[2,128,512]{2,1,0:T(8,128)(2,1)} %copy-done.1, bf16[2,128,512]{2,1,0:T(8,128)(2,1)} %copy-done.2, ...), custom_call_target="tpu_custom_call" | custom-call | tf_op jit(solution)/shard_map/pallas_call | solution.py:415
  97.9 0.7 collective-permute-start.13
  98.8 0.5 copy-done.6
  99.3 18.4 %shard_map.65 = (f32[1,2,1024,256]{3,2,1,0:T(8,128)}, bf16[2,8,128,512]{3,2,1,0:T(8,128)(2,1)}) custom-call(s32[4]{0:T(128)} %refs_0_.5, s32[3]{0:T(128)} %pad_add_fusion.place.refs_1_, bf16[2,8,128,512]{3,2,1,0:T(8,128)(2,1)} %refs_2_.5, bf16[2,128,512]{2,1,0:T(8,128)(2,1)} %copy-done.1, bf16[2,128,512]{2,1,0:T(8,128)(2,1)} %copy-done.2, ...), custom_call_target="tpu_custom_call" | custom-call | tf_op jit(solution)/shard_map/pallas_call | solution.py:415
  117.7 0.9 copy-done.5
  118.7 11.1 %shard_map.66 = bf16[2,8,128,512]{3,2,1,0:T(8,128)(2,1)} custom-call(s32[4]{0:T(128)} %refs_0_.5, s32[3]{0:T(128)} %pad_add_fusion.place.refs_1_, bf16[2,8,128,512]{3,2,1,0:T(8,128)(2,1)} %refs_2_.5, bf16[2,128,512]{2,1,0:T(8,128)(2,1)} %copy-done.1, bf16[2,128,512]{2,1,0:T(8,128)(2,1)} %copy-done.2, ...), custom_call_target="tpu_custom_call", output_to_operand_aliasing={{}: (14, {})} | custom-call | tf_op jit(solution)/shard_map/pallas_call | solution.py:415
  (37 shorter events, 0.5 us)
Async XLA Ops:
  0.0 5.1 %copy-start = (bf16[2,8,128,512]{3,2,1,0:T(8,128)(2,1)S(1)}, bf16[2,8,128,512]{3,2,1,0:T(8,128)(2,1)}, u32[]{:S(2)}) copy-start(bf16[2,8,128,512]{3,2,1,0:T(8,128)(2,1)} %refs_2_.5) | copy-start | bytes 6291460
  4.4 1.8 %copy-start.8 = (f32[8,128]{1,0:T(8,128)S(1)}, f32[8,128]{1,0:T(8,128)}, u32[]{:S(2)}) copy-start(f32[8,128]{1,0:T(8,128)} %local_stats.1) | copy-start | bytes 12292
  4.4 1.8 %collective-permute-start = (f32[8,128]{1,0:T(8,128)}, f32[8,128]{1,0:T(8,128)S(1)}, u32[]{:S(2)}, u32[]{:S(2)}) collective-permute-start(f32[8,128]{1,0:T(8,128)} %local_stats.1), channel_id=1, source_target_pairs={{0,4},{4,0},{8,12},{12,8},{16,20},{20,16},{24,28},{28,24},{1,5},{5... | collective-permute-start | bytes 12296 | tf_op jit(solution)/shard_map/ppermute | solution.py:456
  6.3 5.4 %collective-permute-start.1 = (f32[8,128]{1,0:T(8,128)S(1)}, f32[8,128]{1,0:T(8,128)S(1)}, u32[]{:S(2)}, u32[]{:S(2)}) collective-permute-start(f32[8,128]{1,0:T(8,128)S(1)} %add.35), channel_id=1, source_target_pairs={{0,8},{4,12},{8,0},{12,4},{16,24},{20,28},{24,16},{28,20},{1,9},{5... | collective-permute-start | bytes 12296 | tf_op jit(solution)/shard_map/ppermute | solution.py:456
  8.3 63.3 %collective-permute-start.6 = (bf16[5,128,512]{2,1,0:T(8,128)(2,1)}, bf16[5,128,512]{2,1,0:T(8,128)(2,1)S(1)}, u32[]{:S(2)}, u32[]{:S(2)}) collective-permute-start(bf16[5,128,512]{2,1,0:T(8,128)(2,1)} %dynamic-slice_bitcast_fusion.1), channel_id=1, source_target_pairs={{0,1},{1,2},{2,3},{3,32},{32,33},{33,34},{34,35},{35,64},{64,65},{... | collective-permute-start | bytes 1966088 | tf_op jit(solution)/shard_map/ppermute | solution.py:465
  11.7 2.8 %collective-permute-start.2 = (f32[8,128]{1,0:T(8,128)S(1)}, f32[8,128]{1,0:T(8,128)S(1)}, u32[]{:S(2)}, u32[]{:S(2)}) collective-permute-start(f32[8,128]{1,0:T(8,128)S(1)} %add.36), channel_id=1, source_target_pairs={{0,24},{4,28},{8,16},{12,20},{16,8},{20,12},{24,0},{28,4},{1,25},{... | collective-permute-start | bytes 12296 | tf_op jit(solution)/shard_map/ppermute | solution.py:456
  14.6 7.9 %collective-permute-start.4 = (f32[8,128]{1,0:T(8,128)S(1)}, f32[8,128]{1,0:T(8,128)S(1)}, u32[]{:S(2)}, u32[]{:S(2)}) collective-permute-start(f32[8,128]{1,0:T(8,128)S(1)} %add.37), channel_id=1, source_target_pairs={{0,32},{32,0},{64,96},{96,64},{1,33},{33,1},{65,97},{97,65},{2,34}... | collective-permute-start | bytes 12296 | tf_op jit(solution)/shard_map/ppermute | solution.py:456
  16.2 8.9 %collective-permute-start.3 = (bf16[2,128,512]{2,1,0:T(8,128)(2,1)}, bf16[2,128,512]{2,1,0:T(8,128)(2,1)S(1)}, u32[]{:S(2)}, u32[]{:S(2)}) collective-permute-start(bf16[2,128,512]{2,1,0:T(8,128)(2,1)} %get-tuple-element.15), channel_id=1, source_target_pairs={{0,4},{4,8},{8,12},{12,16},{16,20},{20,24},{24,28},{1,5},{5,9},{9,... | collective-permute-start | bytes 786440 | tf_op jit(solution)/shard_map/ppermute | solution.py:470
  22.5 7.9 %collective-permute-start.5 = (bf16[2,128,512]{2,1,0:T(8,128)(2,1)}, bf16[2,128,512]{2,1,0:T(8,128)(2,1)S(1)}, u32[]{:S(2)}, u32[]{:S(2)}) collective-permute-start(bf16[2,128,512]{2,1,0:T(8,128)(2,1)} %get-tuple-element.16), channel_id=1, source_target_pairs={{4,0},{8,4},{12,8},{16,12},{20,16},{24,20},{28,24},{5,1},{9,5},{13... | collective-permute-start | bytes 786440 | tf_op jit(solution)/shard_map/ppermute | solution.py:472
  25.1 9.9 %copy-start.1 = (bf16[2,128,512]{2,1,0:T(8,128)(2,1)}, bf16[2,128,512]{2,1,0:T(8,128)(2,1)S(1)}, u32[]{:S(2)}) copy-start(bf16[2,128,512]{2,1,0:T(8,128)(2,1)S(1)} %collective-permute-done.3.refs_3_) | copy-start | bytes 786436
  30.4 4.6 %copy-start.2 = (bf16[2,128,512]{2,1,0:T(8,128)(2,1)}, bf16[2,128,512]{2,1,0:T(8,128)(2,1)S(1)}, u32[]{:S(2)}) copy-start(bf16[2,128,512]{2,1,0:T(8,128)(2,1)S(1)} %collective-permute-done.5.refs_4_) | copy-start | bytes 786436
  31.8 66.1 %collective-permute-start.9 = (bf16[6,128,512]{2,1,0:T(8,128)(2,1)S(1)}, bf16[6,128,512]{2,1,0:T(8,128)(2,1)S(1)}, u32[]{:S(2)}, u32[]{:S(2)}) collective-permute-start(bf16[6,128,512]{2,1,0:T(8,128)(2,1)S(1)} %maximum_select_fusion), channel_id=1, source_target_pairs={{0,1},{1,2},{2,3},{3,32},{32,33},{33,34},{34,35},{35,64},{64,65},{... | collective-permute-start | bytes 2359304 | tf_op jit(solution)/shard_map/ppermute | solution.py:485
  35.0 82.7 %collective-permute-start.12 = (bf16[7,128,512]{2,1,0:T(8,128)(2,1)S(1)}, bf16[7,128,512]{2,1,0:T(8,128)(2,1)S(1)}, u32[]{:S(2)}, u32[]{:S(2)}) collective-permute-start(bf16[7,128,512]{2,1,0:T(8,128)(2,1)S(1)} %dynamic-slice_bitcast_fusion), channel_id=1, source_target_pairs={{0,1},{1,2},{2,3},{3,32},{32,33},{33,34},{34,35},{35,64},{64,65},{... | collective-permute-start | bytes 2752520 | tf_op jit(solution)/shard_map/ppermute | solution.py:486
  37.5 3.7 %collective-permute-start.7 = (f32[8,128]{1,0:T(8,128)S(1)}, f32[8,128]{1,0:T(8,128)S(1)}, u32[]{:S(2)}, u32[]{:S(2)}) collective-permute-start(f32[8,128]{1,0:T(8,128)S(1)} %add.38), channel_id=1, source_target_pairs={{0,96},{32,64},{64,32},{96,0},{1,97},{33,65},{65,33},{97,1},{2,98}... | collective-permute-start | bytes 12296 | tf_op jit(solution)/shard_map/ppermute | solution.py:456
  41.3 30.3 %collective-permute-start.8 = (f32[8,128]{1,0:T(8,128)S(1)}, f32[8,128]{1,0:T(8,128)S(1)}, u32[]{:S(2)}, u32[]{:S(2)}) collective-permute-start(f32[8,128]{1,0:T(8,128)S(1)} %add.41), channel_id=1, source_target_pairs={{0,1},{1,0},{2,3},{3,2},{4,5},{5,4},{6,7},{7,6},{8,9},{9,8},{10,11... | collective-permute-start | bytes 12296 | tf_op jit(solution)/shard_map/ppermute | solution.py:456
  71.6 26.3 %copy-start.3 = (bf16[5,128,512]{2,1,0:T(8,128)(2,1)}, bf16[5,128,512]{2,1,0:T(8,128)(2,1)S(1)}, u32[]{:S(2)}) copy-start(bf16[5,128,512]{2,1,0:T(8,128)(2,1)S(1)} %collective-permute-done.6.refs_5_) | copy-start | bytes 1966084
  71.6 4.1 %collective-permute-start.10 = (f32[8,128]{1,0:T(8,128)S(1)}, f32[8,128]{1,0:T(8,128)S(1)}, u32[]{:S(2)}, u32[]{:S(2)}) collective-permute-start(f32[8,128]{1,0:T(8,128)S(1)} %add.42), channel_id=1, source_target_pairs={{0,3},{1,2},{2,1},{3,0},{4,7},{5,6},{6,5},{7,4},{8,11},{9,10},{10,... | collective-permute-start | bytes 12296 | tf_op jit(solution)/shard_map/ppermute | solution.py:484
  71.7 26.9 %collective-permute-start.11 = (bf16[1,128,512]{2,1,0:T(8,128)(2,1)S(1)}, bf16[1,128,512]{2,1,0:T(8,128)(2,1)S(1)}, u32[]{:S(2)}, u32[]{:S(2)}) collective-permute-start(bf16[1,128,512]{2,1,0:T(8,128)(2,1)S(1)} %slice_select_fusion), channel_id=1, source_target_pairs={{0,4},{4,0},{8,12},{12,8},{16,20},{20,16},{24,28},{28,24},{1,5},{5... | collective-permute-start | bytes 393224 | tf_op jit(solution)/shard_map/ppermute | solution.py:483
  97.9 0.9 copy-start.4
  97.9 19.8 %collective-permute-start.13 = (bf16[1,128,512]{2,1,0:T(8,128)(2,1)S(1)}, bf16[1,128,512]{2,1,0:T(8,128)(2,1)S(1)}, u32[]{:S(2)}, u32[]{:S(2)}) collective-permute-start(bf16[1,128,512]{2,1,0:T(8,128)(2,1)S(1)} %slice.59), channel_id=1, source_target_pairs={{0,4},{4,0},{8,12},{12,8},{16,20},{20,16},{24,28},{28,24},{1,5},{5... | collective-permute-start | bytes 393224 | tf_op jit(solution)/shard_map/ppermute | solution.py:497
  98.6 0.6 copy-start.6
  117.7 1.0 copy-start.5
  117.7 1.0 copy-start.7
